TPU v7x, 256 devices: a whole 4x4x8 slice. The times are simulated.
256 devices in a mesh: zslab: 8 (over y_hi, x), xband: 32 (over y_lo, z, core).
Axes of the slice: x: 4, y: 4 (y_hi: 2, y_lo: 2; y = y_hi * 2 + y_lo), z: 8, core: 2. Of those that a mesh axis runs over, the one named last changes fastest.
Arguments:
- volume: float32 [32, 256, 512], P('xband', 'zslab'), may hold values from 0.2 to 1.8
- measured: float32 [32, 256, 512], P('xband', 'zslab'), may hold values from 6.4 to 57.6
- magnification: float32 [32, 32], P(None, 'xband'), may hold values from 1.25 to 2
- shift_y: int32 [32, 32], P(None, 'xband'), may hold values from -32 to 32
- shift_z: int32 [32, 32], P(None, 'xband'), may hold values from -4 to 4
Outputs:
- residual: float32 [32, 256, 512], P('xband', 'zslab')
- correction: float32 [32, 256, 512], P('xband', 'zslab')
All inputs are finite; a program needn't handle non-finite values.
Results may differ from a plain program's by a relative error of at most 0.0003.
Values sent between devices are 32-bit elements; how exact they have to be, the bound alone decides.
A program may use at most 64 MiB of HBM per device.

v0:
```python
import math

import jax
import jax.numpy as jnp
from jax import lax
from jax.sharding import PartitionSpec as P

HALO = 4


def passed_along(x, axis, by):
    devices = lax.axis_size(axis)
    pairs = [(i, i + by) for i in range(devices) if 0 <= i + by < devices]
    return lax.ppermute(x, axis, pairs)


def extended_2(x, sides, width):
    for axis, dim in sides:
        devices, length = (lax.axis_size(axis), x.shape[dim])
        up = [(i, (i + 1) % devices) for i in range(devices - 1)]
        down = [(j, i) for i, j in up]
        last = lax.slice_in_dim(x, length - width, length, axis=dim)
        first = lax.slice_in_dim(x, 0, width, axis=dim)
        before = lax.ppermute(last, axis, up)
        after = lax.ppermute(first, axis, down)
        x = jnp.concatenate([before, x, after], axis=dim)
    return x


def hat_tables(magnification, shift_y, width):
    columns = jnp.arange(width, dtype=jnp.float32)
    centre = (width - 1) / 2.0
    target = (
        (columns[None, None, :] - centre) / magnification[:, :, None]
        + centre
        + shift_y.astype(jnp.float32)[:, :, None]
    )
    return jnp.maximum(0.0, 1.0 - jnp.abs(columns[None, None, None, :] - target[:, :, :, None]))


def split_rims(blocks, depth):
    return (blocks[:, :HALO], blocks[:, HALO : HALO + depth], blocks[:, HALO + depth :])


def shards(volume, measured, magnification, shift_y, shift_z):
    bands, depth, width = volume.shape
    total_x = bands * lax.axis_size("xband")
    total_angles = magnification.shape[0]
    hats = hat_tables(magnification, shift_y, width)

    def forward_rows():
        images = jnp.einsum(
            "izy,aiuy->aizu",
            volume,
            hats,
            precision=lax.Precision.HIGHEST,
            preferred_element_type=jnp.float32,
        )
        padded = jnp.pad(images, ((0, 0), (0, 0), (2 * HALO, 2 * HALO), (0, 0)))

        def place(plane, offset):
            return lax.dynamic_slice_in_dim(plane, HALO - offset, depth + 2 * HALO, 0)

        placed = jax.vmap(jax.vmap(place))(padded, shift_z)
        return jnp.sum(placed, axis=1)

    partial_value = forward_rows()
    lower_rim, middle, upper_rim = split_rims(partial_value, depth)
    from_above = passed_along(lower_rim, "zslab", -1)
    from_below = passed_along(upper_rim, "zslab", 1)
    folded = middle.at[:, depth - HALO :].add(from_above).at[:, :HALO].add(from_below)
    proj = lax.psum_scatter(folded, "xband", scatter_dimension=0, tiled=True)
    measured_sum, proj_sum = lax.psum((jnp.sum(measured, axis=1), jnp.sum(proj, axis=1)), "zslab")
    gain = measured_sum / proj_sum
    residual = (measured - gain[:, None, :] * proj) / total_x
    every = lax.all_gather(residual, "xband", axis=0, tiled=True)
    extended = extended_2(every, (("zslab", 1),), HALO)

    def pick(plane, band_offsets):
        return jax.vmap(lambda offset: lax.dynamic_slice_in_dim(plane, HALO + offset, depth, 0))(
            band_offsets
        )

    rows = jax.vmap(pick)(extended, shift_z)
    images = jnp.einsum(
        "aizu,aiuy->izy",
        rows,
        hats,
        precision=lax.Precision.HIGHEST,
        preferred_element_type=jnp.float32,
    )
    correction = images / math.sqrt(total_angles)
    return (residual, correction)


def solution(mesh):
    return jax.shard_map(
        shards,
        mesh=mesh,
        in_specs=(
            P("xband", "zslab", None),
            P("xband", "zslab", None),
            P(None, "xband"),
            P(None, "xband"),
            P(None, "xband"),
        ),
        out_specs=(P("xband", "zslab", None), P("xband", "zslab", None)),
        check_vma=False,
    )
```

profile of v0, /device:TPU:1, one launch (start us, length us, event | category | flops | bytes accessed | tf_op | source)
XLA Modules:
  0.0 332.9 jit_solution(11127470660264293205)
XLA Ops:
  7.2 0.0 reduce-scatter.2.cloned.1.call-start
  7.2 0.7 convert_bitcast_fusion
  7.9 0.7 fusion.21
  8.6 35.8 %fusion.9 = f32[32,1,32,512]{3,2,0,1:T(8,128)S(1)} fusion(f32[32,512]{1,0:T(8,128)S(1)} %fusion.21, f32[1,32,512]{2,1,0:T(8,128)S(1)} %copy-done), kind=kOutput, calls=%fused_computation.13 | convolution fusion | flops 3254779904 | bytes 2228224 | tf_op jit(solution)/shard_map/izy,aiuy->aizu/dot_general | solution.py:52
  44.4 2.2 copy.17
  46.6 0.1 pad.17.clone
  46.7 0.1 fusion.24
  46.8 2.3 pad.10.clone
  49.2 4.5 %gather_fusion = f32[32,40,512]{2,0,1:T(8,128)} fusion(f32[32,1,48,512]{3,1,0,2:T(1,128)S(1)} %pad.10.clone, s32[32]{0:T(128)S(1)} %or_bitcast_fusion.1), kind=kCustom, calls=%fused_computation | custom fusion | bytes 5243392 | tf_op jit(solution)/shard_map/vmap(vmap())/gather | solution.py:62
  53.7 1.2 fusion.31
  54.9 1.4 collective-permute-start
  56.3 4.6 %collective-permute-start.1 = (f32[32,4,512]{2,0,1:T(8,128)S(1)}, f32[32,4,512]{2,0,1:T(8,128)S(1)}, u32[]{:S(2)}, u32[]{:S(2)}) collective-permute-start(f32[32,4,512]{2,0,1:T(8,128)S(1)} %get-tuple-element.30), channel_id=1, source_target_pairs={{0,32},{32,64},{64,96},{96,128},{128,160},{160,192},{192,224},{1,3... | collective-permute-start | bytes 786440 | tf_op jit(solution)/shard_map/ppermute | solution.py:14
  60.9 1.8 collective-permute-done
  62.8 1.4 collective-permute-done.1
  64.2 0.1 fusion.19
  64.3 2.6 copy.12
  66.8 0.0 reduce-scatter.2.cloned.1.call-update
  66.9 0.0 all-gather.2.cloned.1.call-start
  66.9 125.4 %reduce-scatter.2.cloned.1.call-done = f32[1,32,512]{2,1,0:T(8,128)} async-done(((f32[32,32,512]{2,1,0:T(8,128)}), f32[1,32,512]{2,1,0:T(8,128)}) %reduce-scatter.2.cloned.1.call-update) | async-done | bytes 65552 | tf_op jit(solution)/shard_map/reduce_scatter | solution.py:72
  192.3 0.9 reduce_sum.31
  193.2 19.8 %all-reduce.3 = (f32[1,512]{1,0:T(1,128)S(1)}, f32[1,512]{1,0:T(1,128)S(1)}) all-reduce(f32[1,512]{1,0:T(1,128)S(1)} %bitcast.36, f32[1,512]{1,0:T(1,128)S(1)} %bitcast.37), channel_id=1, replica_groups=mesh['zslab'=8,'xband'=32] {'zslab'}, use_global_device_ids=true, to_apply=%region_1.2 | all-reduce | flops 1024 | bytes 8192 | tf_op jit(solution)/shard_map/psum | solution.py:73
  213.0 1.5 subtract_multiply_fusion
  214.5 0.0 all-gather.2.cloned.1.call-update
  214.5 64.6 %all-gather.2.cloned.1.call-done = f32[32,32,512]{2,1,0:T(8,128)} async-done(((f32[1,32,512]{2,1,0:T(8,128)}), f32[32,32,512]{2,1,0:T(8,128)}) %all-gather.2.cloned.1.call-update) | async-done | bytes 2097168 | tf_op jit(solution)/shard_map/all_gather | solution.py:76
  279.1 2.8 copy.13
  282.0 3.1 collective-permute-start.2
  285.1 1.5 collective-permute-start.3
  286.6 3.8 %collective-permute-done.2 = f32[32,4,512]{2,0,1:T(8,128)S(1)} collective-permute-done((f32[32,4,512]{2,0,1:T(8,128)S(1)}, f32[32,4,512]{2,0,1:T(8,128)S(1)}, u32[]{:S(2)}, u32[]{:S(2)}) %collective-permute-start.2) | collective-permute-done | bytes 262176 | tf_op jit(solution)/shard_map/ppermute | solution.py:24
  290.5 3.8 %collective-permute-done.3 = f32[32,4,512]{2,0,1:T(8,128)S(1)} collective-permute-done((f32[32,4,512]{2,0,1:T(8,128)S(1)}, f32[32,4,512]{2,0,1:T(8,128)S(1)}, u32[]{:S(2)}, u32[]{:S(2)}) %collective-permute-start.3) | collective-permute-done | bytes 262176 | tf_op jit(solution)/shard_map/ppermute | solution.py:25
  294.3 0.3 pad_maximum_fusion
  294.6 4.9 %gather_fusion.1 = f32[32,32,512]{2,0,1:T(8,128)} fusion(f32[32,40,512]{2,0,1:T(8,128)S(1)} %pad_maximum_fusion, s32[32]{0:T(128)S(1)} %or_bitcast_fusion), kind=kCustom, calls=%fused_computation.1 | custom fusion | bytes 4194688 | tf_op jit(solution)/shard_map/vmap(vmap())/gather | solution.py:80
  299.4 26.6 %fusion.16 = f32[1,32,512]{2,1,0:T(8,128)} fusion(f32[32,512]{1,0:T(8,128)S(1)} %fusion.21, f32[32,32,512]{2,0,1:T(8,128)} %gather_fusion.1), kind=kOutput, calls=%fused_computation.16 | convolution fusion | flops 3254796288 | bytes 2228224 | tf_op jit(solution)/shard_map/aizu,aiuy->izy/dot_general | solution.py:85
  (21 shorter events, 0.2 us)
Async XLA Ops:
  7.2 1.5 copy-start
  7.2 185.2 %reduce-scatter.2.cloned.1.call-start = ((), (), s32[]{:S(2)}) async-start(), calls=%async_computation.1 | async-start | bytes 2162688 | tf_op jit(solution)/shard_map/reduce_scatter | solution.py:72
  44.4 2.2 copy-start.3
  53.7 9.1 %copy-start.1 = (f32[32,40,512]{2,0,1:T(8,128)S(1)}, f32[32,40,512]{2,0,1:T(8,128)}, u32[]{:S(2)}) copy-start(f32[32,40,512]{2,0,1:T(8,128)} %gather_fusion) | copy-start | bytes 7864324
  53.7 9.1 %slice-start = ((f32[32,40,512]{2,0,1:T(8,128)}), f32[32,32,512]{2,0,1:T(8,128)S(1)}, s32[]{:S(2)}) async-start(f32[32,40,512]{2,0,1:T(8,128)} %gather_fusion), calls=%async_computation.3 | async-start | bytes 4194304 | tf_op jit(solution)/shard_map/slice | solution.py:42
  54.9 7.8 %collective-permute-start = (f32[32,4,512]{2,0,1:T(8,128)S(1)}, f32[32,4,512]{2,0,1:T(8,128)S(1)}, u32[]{:S(2)}, u32[]{:S(2)}) collective-permute-start(f32[32,4,512]{2,0,1:T(8,128)S(1)} %get-tuple-element.31), channel_id=1, source_target_pairs={{32,0},{64,32},{96,64},{128,96},{160,128},{192,160},{224,192},{33,... | collective-permute-start | bytes 786440 | tf_op jit(solution)/shard_map/ppermute | solution.py:14
  56.3 7.9 %collective-permute-start.1 = (f32[32,4,512]{2,0,1:T(8,128)S(1)}, f32[32,4,512]{2,0,1:T(8,128)S(1)}, u32[]{:S(2)}, u32[]{:S(2)}) collective-permute-start(f32[32,4,512]{2,0,1:T(8,128)S(1)} %get-tuple-element.30), channel_id=1, source_target_pairs={{0,32},{32,64},{64,96},{96,128},{128,160},{160,192},{192,224},{1,3... | collective-permute-start | bytes 786440 | tf_op jit(solution)/shard_map/ppermute | solution.py:14
  64.3 2.6 copy-start.2
  66.9 212.2 %all-gather.2.cloned.1.call-start = ((), (), s32[]{:S(2)}) async-start(), calls=%async_computation.2 | async-start | bytes 2162688 | tf_op jit(solution)/shard_map/all_gather | solution.py:76
  282.0 8.5 %collective-permute-start.2 = (f32[32,4,512]{2,0,1:T(8,128)S(1)}, f32[32,4,512]{2,0,1:T(8,128)S(1)}, u32[]{:S(2)}, u32[]{:S(2)}) collective-permute-start(f32[32,4,512]{2,0,1:T(8,128)S(1)} %get-tuple-element.32), channel_id=1, source_target_pairs={{0,32},{32,64},{64,96},{96,128},{128,160},{160,192},{192,224},{1,3... | collective-permute-start | bytes 786440 | tf_op jit(solution)/shard_map/ppermute | solution.py:24
  285.1 9.2 %collective-permute-start.3 = (f32[32,4,512]{2,0,1:T(8,128)S(1)}, f32[32,4,512]{2,0,1:T(8,128)S(1)}, u32[]{:S(2)}, u32[]{:S(2)}) collective-permute-start(f32[32,4,512]{2,0,1:T(8,128)S(1)} %get-tuple-element.33), channel_id=1, source_target_pairs={{32,0},{64,32},{96,64},{128,96},{160,128},{192,160},{224,192},{33,... | collective-permute-start | bytes 786440 | tf_op jit(solution)/shard_map/ppermute | solution.py:25
Sparse Core Ops, SparseCore 0:
  67.0 125.3 reduce-scatter.1
  214.6 64.4 all-gather.1
where the time goes:
time: 338 us; the launch traced here: 333 us
  waiting for transfers between devices  201 us (59%)
  matrix products  62.4 us (18%)
  local copies, waits for them, and re-layouts  20.6 us (6%)
  blocking collectives  19.8 us (6%)
  between operations  14.2 us (4%)
  starting transfers between devices  10.7 us (3%)
  other arithmetic  4.26 us (1%)
    reduce_scatter x1, waiting for transfers between devices, shards(): proj = lax.psum_scatter(folded, 'xband', scatter_dimension=0, tiled=True)  125 us
    all_gather x1, waiting for transfers between devices, shards(): every = lax.all_gather(residual, 'xband', axis=0, tiled=True)  64.6 us
    dot_general x1, matrix products, forward_rows(): jnp.einsum('izy,aiuy->aizu', volume, hats, precision=lax.Precision.HIGHES...  35.8 us
    dot_general x1, matrix products, shards(): jnp.einsum('aizu,aiuy->izy', rows, hats, precision=lax.Precision.HIGHEST,...  26.6 us
    psum x1, blocking collectives, shards(): lax.psum((jnp.sum(measured, axis=1), jnp.sum(proj, axis=1)), 'zslab')  19.8 us
  transfers between devices with their start and end apart: 6, of which 6 were waited for; matrix products, arithmetic and copies ran while one was open for 0% of the time, Pallas kernels for 0%

commit v1 on v0

v1 whole, which is shorter than its diff:
```python
import math

import jax
import jax.numpy as jnp
from jax import lax
from jax.experimental import pallas as pl
from jax.experimental.pallas import tpu as pltpu
from jax.sharding import PartitionSpec as P

HALO = 4
TILES = 4
ROWS = 32
EXT = ROWS + 2 * HALO
SLABS = 8
RING = 8
BANDS = 32
CENTRE = 255.5
VOL_ROWS = TILES * ROWS + 8
RES_ROWS = TILES * EXT
VOL_A, VOL_B, VOL_ALL = (0, 64), (64, 72), (0, 136)
RES_A, RES_B, RES_ALL = (0, 80), (80, 80), (0, 160)
COPIES = 46
FORWARD_TILES = ((0, 1), (0, 1, 2), (1, 2, 3), (2, 3))
BACKWARD_TILES = ((0,), (0, 1), (0, 1), (1,))
MESH = pl.DeviceIdType.MESH


def take(x, index):
    return jnp.take_along_axis(x, index, axis=1, mode="promise_in_bounds")


def iota(axis):
    return lax.broadcasted_iota(jnp.int32, (8, 128), axis)


def project_block(blocks, slot, mag, offset, shift, work, total):
    lane = iota(1)
    mag = jnp.full((8, 128), mag, jnp.float32)
    for ub in range(TILES):
        u = (lane + 128 * ub).astype(jnp.float32)
        target = (u - CENTRE) / mag + CENTRE + offset
        lower = jnp.floor(target)
        frac = target - lower
        left = lower.astype(jnp.int32)
        right = left + 1
        left_lane, right_lane = left & 127, right & 127
        tiles = FORWARD_TILES[ub]
        for rg in range(ROWS // 8):
            x = [blocks[slot, ROWS * k + 8 * rg : ROWS * k + 8 * rg + 8, :] for k in tiles]
            a, b = take(x[0], left_lane), take(x[0], right_lane)
            for k, tile in zip(tiles[1:], x[1:]):
                a = jnp.where(left >= 128 * k, take(tile, left_lane), a)
                b = jnp.where(right >= 128 * k, take(tile, right_lane), b)
            work[ub, 8 + 8 * rg : 16 + 8 * rg, :] = (1.0 - frac) * a + frac * b
    for ub in range(TILES):
        for rg in range(EXT // 8):
            moved = work[ub, pl.ds(8 + 8 * rg - HALO - shift, 8), :]
            total[ub][rg] = total[ub][rg] + moved


def tap_tables(mag, offset, index_ref, weight_ref, angle):
    lane = iota(1)
    mag = jnp.full((8, 128), mag, jnp.float32)
    for yb in range(TILES):
        y = (lane + 128 * yb).astype(jnp.float32)
        middle = (y - CENTRE - offset) * mag + CENTRE
        for phase in range(2):
            first = jnp.floor((middle - phase) * 0.5).astype(jnp.int32)
            for tap in range(2):
                j = first + tap
                u = (2 * j + phase).astype(jnp.float32)
                target = (u - CENTRE) / mag + CENTRE + offset
                weight = jnp.maximum(0.0, 1.0 - jnp.abs(y - target))
                weight = jnp.where((j >= 0) & (j < 256), weight, 0.0)
                n = 8 * (yb * 4 + phase * 2 + tap)
                index_ref[angle, n : n + 8, :] = jnp.clip(j, 0, 255)
                weight_ref[angle, n : n + 8, :] = weight


def backproject_block(blocks, slot, angle, shift, index_ref, weight_ref, work, total):
    for n in range(0, RES_ROWS, 8):
        work[n : n + 8, :] = blocks[slot, n : n + 8, :]
    for yb in range(TILES):
        n = 32 * yb
        index = [index_ref[angle, n + 8 * t : n + 8 * t + 8, :] for t in range(4)]
        weight = [weight_ref[angle, n + 8 * t : n + 8 * t + 8, :] for t in range(4)]
        lanes = [j & 127 for j in index]
        tiles = BACKWARD_TILES[yb]
        for rg in range(ROWS // 8):
            for phase in range(2):
                start = EXT * phase + HALO + 8 * rg + shift
                x = [work[pl.ds(start + 2 * EXT * k, 8), :] for k in tiles]
                for t in (2 * phase, 2 * phase + 1):
                    value = take(x[0], lanes[t])
                    if len(tiles) == 2:
                        value = jnp.where(index[t] >= 128, take(x[1], lanes[t]), value)
                    total[yb][rg] = total[yb][rg] + weight[t] * value


class Gather:
    def __init__(self, blocks, half_a, half_b, whole, send, recv, place):
        self.blocks, self.send_sem, self.recv_sem = blocks, send, recv
        self.parts = (half_a, half_b, half_a)
        self.half_a, self.half_b, self.whole = half_a, half_b, whole
        self.place = place
        self.sent = []

    def copy(self, source, target, part, n, to):
        rows = pl.ds(*part)
        return pltpu.make_async_remote_copy(
            src_ref=self.blocks.at[source, rows],
            dst_ref=self.blocks.at[target, rows],
            send_sem=self.send_sem.at[n],
            recv_sem=self.recv_sem.at[n],
            device_id={"xband": self.place[to]},
            device_id_type=MESH,
        )

    def send(self, source, target, part, n, to):
        copy = self.copy(source, target, part, n, to)
        copy.start()
        self.sent.append(copy)

    def wait(self, slot, part, n, to):
        self.copy(slot, slot, part, n, to).wait_recv()

    def along(self, way, step, p):
        base = 0 if way == "long" else 4
        source = 0 if step == 0 else base + step
        side = 8 if p == 2 else 0
        n = (0 if way == "long" else 12) + 3 * step + p
        self.send(source + side, base + step + 1 + side, self.parts[p], n, way)

    def start(self):
        self.send(0, 8, self.half_a, 21, "pair")
        self.along("long", 0, 0)
        self.along("short", 0, 0)
        self.along("long", 0, 1)
        self.along("short", 0, 1)
        self.send(0, 8, self.half_b, 22, "pair")
        self.send(0, 16, self.whole, 30, "core")

    def run(self, arrived, group):
        arrived(0)
        self.wait(8, self.half_a, 21, "pair")
        self.along("long", 0, 2)
        self.along("short", 0, 2)
        groups = ((0,), (1, 5), (2, 6), (3, 7), (4,))
        for step in range(1, 7):
            if 2 <= step:
                for r in groups[step - 2]:
                    for side in (0, 8):
                        self.wait(16 + side + r, self.whole, 30 + side + r, "core")
                        arrived(16 + side + r)
            if step <= 4:
                for r in groups[step]:
                    way, last = ("long", 4) if r <= 4 else ("short", 3)
                    first = (0 if r <= 4 else 12) + 3 * (step - 1)
                    for p in range(3):
                        self.wait(r + (8 if p == 2 else 0), self.parts[p], first + p, way)
                        if step < last:
                            self.along(way, step, p)
                        if p == 1:
                            self.send(r, 8 + r, self.half_b, 22 + r, "pair")
                            self.send(r, 16 + r, self.whole, 30 + r, "core")
                            arrived(r)
            if step <= 5:
                for r in groups[step - 1]:
                    self.wait(8 + r, self.half_b, 22 + r, "pair")
                    self.send(8 + r, 24 + r, self.whole, 38 + r, "core")
                    arrived(8 + r)
            if 2 <= step:
                for r in groups[step - 2]:
                    group(r)

    def finish(self):
        for copy in self.sent:
            copy.wait_send()


def load_total(ref, rows):
    return [[ref[t, 8 * g : 8 * g + 8, :] for g in range(rows // 8)] for t in range(TILES)]


def store_total(ref, total):
    for t, groups in enumerate(total):
        for g, value in enumerate(groups):
            ref[t, 8 * g : 8 * g + 8, :] = value


def kernel(
    mag_ref, offset_ref, shift_ref, volume_ref, measured_ref, residual_ref, correction_ref,
    vols, ress, tables, seen, proj, ext, back, sums, below, above, index_ref, weight_ref, image, rows,
    vol_send, vol_recv, res_send, res_recv, slab_send, slab_recv, table_sem,
):
    slab, band = lax.axis_index("zslab"), lax.axis_index("xband")
    half, core = lax.div(band, 16), lax.rem(band, 2)
    z = lax.div(lax.rem(band, 16), 2)
    turn = 1 - 2 * core

    def band_of(half, z, core):
        return half * 16 + lax.rem(z + 2 * RING, RING) * 2 + core

    place = {
        "long": band_of(half, z + turn, core),
        "short": band_of(half, z - turn, core),
        "pair": band_of(1 - half, z, core),
        "core": band_of(half, z, 1 - core),
    }
    barrier = pltpu.get_barrier_semaphore()
    for to in place.values():
        pl.semaphore_signal(barrier, inc=1, device_id={"xband": to}, device_id_type=MESH)
    slabs = [lax.rem(slab + j, SLABS) for j in range(SLABS)]
    for to in slabs[1:]:
        pl.semaphore_signal(barrier, inc=1, device_id={"zslab": to}, device_id_type=MESH)

    lane, row = iota(1), iota(0)

    def spread(angle, values):
        here = lane == angle
        mags, offsets, shifts = values
        return (
            jnp.where(here, mag_ref[angle], mags),
            jnp.where(here, offset_ref[angle].astype(jnp.float32), offsets),
            jnp.where(here, shift_ref[angle].astype(jnp.float32), shifts),
        )

    zeros = jnp.zeros((8, 128), jnp.float32)
    mags, offsets, shifts = lax.fori_loop(0, BANDS, spread, (zeros, zeros, zeros))
    for t in range(TILES):
        vols[0, ROWS * t : ROWS * (t + 1), :] = volume_ref[0, :, 128 * t : 128 * (t + 1)]
        seen[t, 8 : 8 + ROWS, :] = measured_ref[0, :, 128 * t : 128 * (t + 1)]
    vols[0, VOL_ROWS - 8 :, :] = jnp.where(row == 0, mags, jnp.where(row == 1, offsets, shifts))

    pl.semaphore_wait(barrier, 4 + SLABS - 1)

    gather = Gather(vols, VOL_A, VOL_B, VOL_ALL, vol_send, vol_recv, place)
    gather.start()

    def slab_copy(source, target, n, to):
        return pltpu.make_async_remote_copy(
            src_ref=source,
            dst_ref=target,
            send_sem=slab_send.at[n],
            recv_sem=slab_recv.at[n],
            device_id={"zslab": slabs[to]},
            device_id_type=MESH,
        )

    seen_up = slab_copy(seen.at[:, pl.ds(ROWS, 8)], seen.at[:, pl.ds(0, 8)], 0, 1)
    seen_down = slab_copy(seen.at[:, pl.ds(8, 8)], seen.at[:, pl.ds(ROWS + 8, 8)], 1, SLABS - 1)
    seen_up.start()
    seen_down.start()

    for t in range(TILES):
        image[t, 0:8, :] = zeros
        image[t, 8 + ROWS :, :] = zeros
        proj[t] = jnp.zeros((EXT, 128), jnp.float32)
        back[t] = jnp.zeros((ROWS, 128), jnp.float32)

    def fill(angle, carry):
        tap_tables(mag_ref[angle], offset_ref[angle].astype(jnp.float32), index_ref, weight_ref, angle)
        return carry

    lax.fori_loop(0, BANDS, fill, 0)

    def table_copy(slot):
        return pltpu.make_async_copy(
            vols.at[slot, pl.ds(VOL_ROWS - 8, 8)], tables.at[slot], table_sem.at[slot]
        )

    def project_group(r):
        for j in range(4):
            table_copy(r + 8 * j).wait()

        def one(j, carry):
            slot = r + 8 * j
            total = load_total(proj, EXT)
            project_block(
                vols, slot, tables[slot, 0, band], tables[slot, 1, band],
                jnp.clip(tables[slot, 2, band].astype(jnp.int32), -HALO, HALO), image, total,
            )
            store_total(proj, total)
            return carry

        lax.fori_loop(0, 4, one, 0)

    gather.run(lambda slot: table_copy(slot).start(), project_group)

    for t in range(TILES):
        column = jnp.zeros((1, 128), jnp.float32)
        for g in range(EXT // 8):
            value = proj[t, 8 * g : 8 * g + 8, :]
            if g == 0:
                value = jnp.where(row + slab * ROWS >= HALO, value, 0.0)
            if g == EXT // 8 - 1:
                value = jnp.where((row < HALO) | (slab < SLABS - 1), value, 0.0)
            column = column + jnp.sum(value, axis=0, keepdims=True)
        sums[0, t : t + 1, :] = column
        sums[0, TILES + t : TILES + t + 1, :] = jnp.sum(seen[t, 8 : 8 + ROWS, :], axis=0, keepdims=True)
    slab_copies = [seen_up, seen_down]
    for j in range(1, SLABS):
        slab_copies.append(slab_copy(sums.at[0], sums.at[j], 3 + j, j))
    slab_copies.append(slab_copy(proj.at[:, pl.ds(ROWS, 8)], below, 2, 1))
    slab_copies.append(slab_copy(proj.at[:, pl.ds(0, 8)], above, 3, SLABS - 1))
    for copy in slab_copies[2:]:
        copy.start()
    for copy in slab_copies:
        copy.wait_recv()

    all_sums = sums[0]
    for j in range(1, SLABS):
        all_sums = all_sums + sums[j]
    for t in range(TILES):
        gain = all_sums[TILES + t : TILES + t + 1, :] / all_sums[t : t + 1, :]
        gain = jnp.broadcast_to(gain, (8, 128))
        for g in range(EXT // 8):
            value = proj[t, 8 * g : 8 * g + 8, :]
            if g == 0:
                value = value + jnp.where(slab > 0, below[t], 0.0)
            if g == EXT // 8 - 1:
                value = value + jnp.where(slab < SLABS - 1, above[t], 0.0)
            value = (seen[t, 8 * g + HALO : 8 * g + HALO + 8, :] - gain * value) * (1.0 / BANDS)
            if g == 0:
                value = jnp.where(row + slab * ROWS >= HALO, value, 0.0)
            if g == EXT // 8 - 1:
                value = jnp.where((row < HALO) | (slab < SLABS - 1), value, 0.0)
            ext[t, 8 * g : 8 * g + 8, :] = value
    double = 2 * (lane & 63)
    for k in range(2):
        for phase in range(2):
            for g in range(EXT // 8):
                a = take(ext[2 * k, 8 * g : 8 * g + 8, :], double + phase)
                b = take(ext[2 * k + 1, 8 * g : 8 * g + 8, :], double + phase)
                first = 2 * EXT * k + EXT * phase + 8 * g
                ress[0, first : first + 8, :] = jnp.where(lane < 64, a, b)

    spread_out = Gather(ress, RES_A, RES_B, RES_ALL, res_send, res_recv, place)
    spread_out.start()
    for t in range(TILES):
        residual_ref[0, :, 128 * t : 128 * (t + 1)] = ext[t, HALO : HALO + ROWS, :]

    def backproject_group(r):
        away = 0 if r == 0 else (-r if r <= 4 else r - 4)

        def one(j, carry):
            side, plane = lax.rem(j, 2), lax.div(j, 2)
            from_half = half + side - 2 * half * side
            from_core = core + plane - 2 * core * plane
            angle = band_of(from_half, z + away * (1 - 2 * from_core), from_core)
            total = load_total(back, ROWS)
            backproject_block(ress, r + 8 * j, angle, shift_ref[angle], index_ref, weight_ref, rows, total)
            store_total(back, total)
            return carry

        lax.fori_loop(0, 4, one, 0)

    spread_out.run(lambda slot: None, backproject_group)
    for t in range(TILES):
        correction_ref[0, :, 128 * t : 128 * (t + 1)] = back[t] * (1.0 / math.sqrt(BANDS))
    gather.finish()
    spread_out.finish()
    for copy in slab_copies:
        copy.wait_send()


def shards(volume, measured, magnification, shift_y, shift_z):
    smem, vmem = pl.BlockSpec(memory_space=pltpu.SMEM), pl.BlockSpec(memory_space=pltpu.VMEM)
    block = jax.ShapeDtypeStruct(volume.shape, jnp.float32)
    f32 = jnp.float32
    return pl.pallas_call(
        kernel,
        out_shape=(block, block),
        in_specs=[smem, smem, smem, vmem, vmem],
        out_specs=(vmem, vmem),
        scratch_shapes=[
            pltpu.VMEM((BANDS, VOL_ROWS, 128), f32),
            pltpu.VMEM((BANDS, RES_ROWS, 128), f32),
            pltpu.SMEM((BANDS, 8, 128), f32),
            pltpu.VMEM((TILES, ROWS + 16, 128), f32),
            pltpu.VMEM((TILES, EXT, 128), f32),
            pltpu.VMEM((TILES, EXT, 128), f32),
            pltpu.VMEM((TILES, ROWS, 128), f32),
            pltpu.VMEM((SLABS, 8, 128), f32),
            pltpu.VMEM((TILES, 8, 128), f32),
            pltpu.VMEM((TILES, 8, 128), f32),
            pltpu.VMEM((BANDS, 128, 128), jnp.int32),
            pltpu.VMEM((BANDS, 128, 128), f32),
            pltpu.VMEM((TILES, ROWS + 16, 128), f32),
            pltpu.VMEM((RES_ROWS, 128), f32),
            pltpu.SemaphoreType.DMA((COPIES,)),
            pltpu.SemaphoreType.DMA((COPIES,)),
            pltpu.SemaphoreType.DMA((COPIES,)),
            pltpu.SemaphoreType.DMA((COPIES,)),
            pltpu.SemaphoreType.DMA((SLABS + 3,)),
            pltpu.SemaphoreType.DMA((SLABS + 3,)),
            pltpu.SemaphoreType.DMA((BANDS,)),
        ],
        compiler_params=pltpu.CompilerParams(
            collective_id=0, has_side_effects=True, vmem_limit_bytes=40 * 1024 * 1024
        ),
        name="sirt",
    )(
        magnification.reshape(BANDS),
        shift_y.reshape(BANDS),
        shift_z.reshape(BANDS),
        volume,
        measured,
    )


def solution(mesh):
    return jax.shard_map(
        shards,
        mesh=mesh,
        in_specs=(
            P("xband", "zslab", None),
            P("xband", "zslab", None),
            P(None, "xband"),
            P(None, "xband"),
            P(None, "xband"),
        ),
        out_specs=(P("xband", "zslab", None), P("xband", "zslab", None)),
        check_vma=False,
    )
```

time: 338 us -> 68.3 us (0.20); the launches traced: 333 us -> 68.1 us
  waiting for transfers between devices: 201 us -> 0 us
  Pallas kernels: 0 us -> 63.9 us
  matrix products: 62.4 us -> 0 us
  blocking collectives: 19.8 us -> 0 us
  local copies, waits for them, and re-layouts: 20.6 us -> 3.6 us
  between operations: 14.2 us -> 0.67 us
  starting transfers between devices: 10.7 us -> 0 us
  other arithmetic: 4.26 us -> 0 us
    reduce_scatter x1 -> x0, waiting for transfers between devices: 125 us -> none  [shards(): proj = lax.psum_scatter(folded, 'xband', scatter_dimension=0, tiled=True)]
    all_gather x1 -> x0, waiting for transfers between devices: 64.6 us -> none  [shards(): every = lax.all_gather(residual, 'xband', axis=0, tiled=True)]
    pallas_call x0 -> x1, Pallas kernels: none -> 63.9 us  [shards(): pl.pallas_call(kernel, out_shape=(block, block), in_specs=[smem, smem, sm...]
    dot_general x2 -> x0, matrix products: 62.4 us -> none  [the longest x1 35.8 us: forward_rows(): jnp.einsum('izy,aiuy->aizu', volume, hats, precision=lax.Precision.HIGHES...]
    psum x1 -> x0, blocking collectives: 19.8 us -> none  [shards(): lax.psum((jnp.sum(measured, axis=1), jnp.sum(proj, axis=1)), 'zslab')]
    ppermute x4 -> x0, waiting for transfers between devices: 10.9 us -> none  [the longest x1 3.83 us: extended_2(): before = lax.ppermute(last, axis, up)]
    ppermute x4 -> x0, starting transfers between devices: 10.6 us -> none  [the longest x2 6.01 us: passed_along(): return lax.ppermute(x, axis, pairs)]
    gather x3 -> x0, local copies, waits for them, and re-layouts: 9.45 us -> none  [the longest x1 4.87 us: pick(): lax.dynamic_slice_in_dim(plane, HALO + offset, depth, 0)]
  transfers between devices with their start and end apart: 6 -> 0, of which waited for: 6 -> 0; matrix products, arithmetic and copies ran while one was open for 0% -> 0% of each run, Pallas kernels for 0% -> 0%
where the time goes in v1:
time: 68.3 us; the launch traced here: 68.1 us
  Pallas kernels  63.9 us (94%)
  local copies, waits for them, and re-layouts  3.6 us (5%)
    pallas_call x1, Pallas kernels, shards(): pl.pallas_call(kernel, out_shape=(block, block), in_specs=[smem, smem, sm...  63.9 us
    unnamed x12, local copies, waits for them, and re-layouts  3.6 us

profile of v1, /device:TPU:1, one launch (start us, length us, event | category | flops | bytes accessed | tf_op | source)
XLA Modules:
  0.0 68.1 jit_solution(14251613894811226889)
XLA Ops:
  0.6 0.0 copy-start.2
  0.6 0.0 copy-start.3
  0.7 0.0 copy-start.4
  0.7 0.6 copy-done.2
  1.3 0.0 copy-done.3
  1.3 0.0 copy-done.4
  1.3 0.0 copy-start
  1.3 0.8 %copy-done = f32[1,32,512]{2,1,0:T(8,128)S(1)} copy-done((f32[1,32,512]{2,1,0:T(8,128)S(1)}, f32[1,32,512]{2,1,0:T(8,128)}, u32[]{:S(2)}) %copy-start) | copy-done | bytes 65560
  2.2 0.0 copy-start.1
  2.2 0.8 %copy-done.1 = f32[1,32,512]{2,1,0:T(8,128)S(1)} copy-done((f32[1,32,512]{2,1,0:T(8,128)S(1)}, f32[1,32,512]{2,1,0:T(8,128)}, u32[]{:S(2)}) %copy-start.1) | copy-done | bytes 65560
  3.0 63.9 %sirt.1 = (f32[1,32,512]{2,1,0:T(8,128)S(1)}, f32[1,32,512]{2,1,0:T(8,128)S(1)}) custom-call(f32[32]{0:T(128)S(1)} %bitcast.3, s32[32]{0:T(128)S(1)} %bitcast.4, s32[32]{0:T(128)S(1)} %bitcast.5, f32[1,32,512]{2,1,0:T(8,128)S(1)} %copy-done, f32[1,32,512]{2,1,0:T(8,128)S(1)} %copy-done.1), custom_call_target="tpu_custom_call" | custom-call | tf_op jit(solution)/shard_map/sirt/pallas_call | solution.py:371
  66.9 0.6 copy.9
  67.5 0.6 copy.10
Async XLA Ops:
  0.6 0.7 copy-start.2
  0.6 0.7 copy-start.3
  0.7 0.7 copy-start.4
  1.3 0.8 %copy-start = (f32[1,32,512]{2,1,0:T(8,128)S(1)}, f32[1,32,512]{2,1,0:T(8,128)}, u32[]{:S(2)}) copy-start(f32[1,32,512]{2,1,0:T(8,128)} %volume_ref.1) | copy-start | bytes 196612
  2.2 0.8 %copy-start.1 = (f32[1,32,512]{2,1,0:T(8,128)S(1)}, f32[1,32,512]{2,1,0:T(8,128)}, u32[]{:S(2)}) copy-start(f32[1,32,512]{2,1,0:T(8,128)} %measured_ref.1) | copy-start | bytes 196612

commit v2 on v1

v2 whole, which is shorter than its diff:
```python
import math

import jax
import jax.numpy as jnp
from jax import lax
from jax.experimental import pallas as pl
from jax.experimental.pallas import tpu as pltpu
from jax.sharding import PartitionSpec as P

HALO = 4
TILES = 4
ROWS = 32
EXT = ROWS + 2 * HALO
SLABS = 8
RING = 8
BANDS = 32
CENTRE = 255.5
VOL_ROWS = TILES * ROWS + 8
RES_ROWS = TILES * EXT
VOL_PARTS = ((0, 64), (64, 72), (0, 136))
RES_PARTS = ((0, 80), (80, 80), (0, 160))
COPIES = 20
COLUMN = 16
FORWARD_TILES = ((0, 1), (0, 1, 2), (1, 2, 3), (2, 3))
BACKWARD_TILES = ((0,), (0, 1), (0, 1), (1,))
MESH = pl.DeviceIdType.MESH


def take(x, index):
    return jnp.take_along_axis(x, index, axis=1, mode="promise_in_bounds")


def iota(axis):
    return lax.broadcasted_iota(jnp.int32, (8, 128), axis)


def project_block(blocks, slot, mag, offset, shift, work, total):
    lane = iota(1)
    mag = jnp.full((8, 128), mag, jnp.float32)
    for ub in range(TILES):
        u = (lane + 128 * ub).astype(jnp.float32)
        target = (u - CENTRE) / mag + CENTRE + offset
        lower = jnp.floor(target)
        frac = target - lower
        left = lower.astype(jnp.int32)
        right = left + 1
        left_lane, right_lane = left & 127, right & 127
        tiles = FORWARD_TILES[ub]
        for rg in range(ROWS // 8):
            x = [blocks[slot, ROWS * k + 8 * rg : ROWS * k + 8 * rg + 8, :] for k in tiles]
            a, b = take(x[0], left_lane), take(x[0], right_lane)
            for k, tile in zip(tiles[1:], x[1:]):
                a = jnp.where(left >= 128 * k, take(tile, left_lane), a)
                b = jnp.where(right >= 128 * k, take(tile, right_lane), b)
            work[ub, 8 + 8 * rg : 16 + 8 * rg, :] = (1.0 - frac) * a + frac * b
    for ub in range(TILES):
        for rg in range(EXT // 8):
            moved = work[ub, pl.ds(8 + 8 * rg - HALO - shift, 8), :]
            total[ub][rg] = total[ub][rg] + moved


def tap_tables(mag, offset, index_ref, weight_ref, angle):
    lane = iota(1)
    mag = jnp.full((8, 128), mag, jnp.float32)
    for yb in range(TILES):
        y = (lane + 128 * yb).astype(jnp.float32)
        middle = (y - CENTRE - offset) * mag + CENTRE
        for phase in range(2):
            first = jnp.floor((middle - phase) * 0.5).astype(jnp.int32)
            for tap in range(2):
                j = first + tap
                u = (2 * j + phase).astype(jnp.float32)
                target = (u - CENTRE) / mag + CENTRE + offset
                weight = jnp.maximum(0.0, 1.0 - jnp.abs(y - target))
                weight = jnp.where((j >= 0) & (j < 256), weight, 0.0)
                n = 8 * (yb * 4 + phase * 2 + tap)
                index_ref[angle, n : n + 8, :] = jnp.clip(j, 0, 255)
                weight_ref[angle, n : n + 8, :] = weight


def backproject_block(blocks, slot, angle, shift, index_ref, weight_ref, work, total):
    for n in range(0, RES_ROWS, 8):
        work[n : n + 8, :] = blocks[slot, n : n + 8, :]
    for yb in range(TILES):
        n = 32 * yb
        index = [index_ref[angle, n + 8 * t : n + 8 * t + 8, :] for t in range(4)]
        weight = [weight_ref[angle, n + 8 * t : n + 8 * t + 8, :] for t in range(4)]
        lanes = [j & 127 for j in index]
        tiles = BACKWARD_TILES[yb]
        for rg in range(ROWS // 8):
            for phase in range(2):
                start = EXT * phase + HALO + 8 * rg + shift
                x = [work[pl.ds(start + 2 * EXT * k, 8), :] for k in tiles]
                for t in (2 * phase, 2 * phase + 1):
                    value = take(x[0], lanes[t])
                    if len(tiles) == 2:
                        value = jnp.where(index[t] >= 128, take(x[1], lanes[t]), value)
                    total[yb][rg] = total[yb][rg] + weight[t] * value


class Gather:
    def __init__(self, blocks, parts, send, recv, place):
        self.blocks, self.parts, self.send_sem, self.recv_sem = blocks, parts, send, recv
        self.place = place
        self.sent = []

    def copy(self, source, target, part, n, to):
        rows = pl.ds(*self.parts[part])
        return pltpu.make_async_remote_copy(
            src_ref=self.blocks.at[source, rows],
            dst_ref=self.blocks.at[target, rows],
            send_sem=self.send_sem.at[n],
            recv_sem=self.recv_sem.at[n],
            device_id={"xband": self.place[to]},
            device_id_type=MESH,
        )

    def send(self, source, target, part, n, to):
        copy = self.copy(source, target, part, n, to)
        copy.start()
        self.sent.append(copy)

    def wait(self, slot, part, n):
        self.copy(slot, slot, part, n, "core").wait_recv()

    def start(self):
        for part in range(2):
            self.send(0, 2, part, 2 + part, "long2")
            self.send(0, 6, part, 4 + part, "short2")
        self.send(0, 1, 2, 0, "long1")
        self.send(0, 5, 2, 1, "short1")
        self.send(0, 8, 2, 12, "core")

    def core(self, r):
        self.send(r, 8 + r, 2, 12 + r, "core")

    def run(self, arrived, compute, meanwhile):
        arrived(0)
        compute(0)
        self.wait(8, 2, 12)
        arrived(8)
        compute(8)
        for part in range(2):
            self.wait(2, part, 2 + part)
            self.send(2, 4, part, 8 + part, "long2")
            self.send(2, 3, part, 6 + part, "long1")
            self.wait(6, part, 4 + part)
            self.send(6, 7, part, 10 + part, "short1")
        self.core(2)
        self.core(6)
        for n, r in enumerate((1, 5)):
            self.wait(r, 2, n)
            self.core(r)
        for r in (1, 5, 2, 6):
            arrived(r)
        meanwhile()
        for r in (1, 5, 2, 6):
            compute(r)
        for r in (2, 6, 1, 5):
            self.wait(8 + r, 2, 12 + r)
            arrived(8 + r)
        for r in (9, 13):
            compute(r)
        for r, n in ((3, 6), (7, 10), (4, 8)):
            self.wait(r, 0, n)
            self.wait(r, 1, n + 1)
            self.core(r)
            arrived(r)
        for r in (10, 14, 3, 7, 4):
            compute(r)
        for r in (3, 7, 4):
            self.wait(8 + r, 2, 12 + r)
            arrived(8 + r)
        for r in (11, 15, 12):
            compute(r)

    def finish(self):
        for copy in self.sent:
            copy.wait_send()


def load_total(ref, q, rows):
    return [[ref[q, t, 8 * g : 8 * g + 8, :] for g in range(rows // 8)] for t in range(TILES)]


def store_total(ref, q, total):
    for t, groups in enumerate(total):
        for g, value in enumerate(groups):
            ref[q, t, 8 * g : 8 * g + 8, :] = value


def kernel(
    mag_ref, offset_ref, shift_ref, volume_ref, measured_ref, residual_ref, correction_ref,
    vols, ress, tables, pair_vmem, pair_ref, seen, proj, other, ext, back, other_back, own_sums, sums, below, above,
    index_ref, weight_ref, image, rows,
    vol_send, vol_recv, res_send, res_recv, slab_send, slab_recv, pair_send, pair_recv, table_sem,
):
    slab, band = lax.axis_index("zslab"), lax.axis_index("xband")
    half, core = lax.div(band, 16), lax.rem(band, 2)
    z = lax.div(lax.rem(band, 16), 2)
    turn = 1 - 2 * core
    pair = (1 - half) * COLUMN + lax.rem(band, COLUMN)

    def ring(away):
        return half * COLUMN + lax.rem(z + away + 2 * RING, RING) * 2 + core

    place = {
        "long1": ring(turn),
        "long2": ring(2 * turn),
        "short1": ring(-turn),
        "short2": ring(-2 * turn),
        "core": band + turn,
        "pair": pair,
    }
    barrier = pltpu.get_barrier_semaphore()
    for to in place.values():
        pl.semaphore_signal(barrier, inc=1, device_id={"xband": to}, device_id_type=MESH)
    slabs = [lax.rem(slab + j, SLABS) for j in range(SLABS)]
    for to in slabs[1:]:
        for of in (band, pair):
            pl.semaphore_signal(barrier, inc=1, device_id={"zslab": to, "xband": of}, device_id_type=MESH)

    lane, row = iota(1), iota(0)

    def spread(angle, values):
        here = lane == angle
        mags, offsets, shifts = values
        return (
            jnp.where(here, mag_ref[angle], mags),
            jnp.where(here, offset_ref[angle].astype(jnp.float32), offsets),
            jnp.where(here, shift_ref[angle].astype(jnp.float32), shifts),
        )

    zeros = jnp.zeros((8, 128), jnp.float32)
    mags, offsets, shifts = lax.fori_loop(0, BANDS, spread, (zeros, zeros, zeros))
    for t in range(TILES):
        vols[0, ROWS * t : ROWS * (t + 1), :] = volume_ref[0, :, 128 * t : 128 * (t + 1)]
        seen[t, 8 : 8 + ROWS, :] = measured_ref[0, :, 128 * t : 128 * (t + 1)]
    vols[0, VOL_ROWS - 8 :, :] = jnp.where(row == 0, mags, jnp.where(row == 1, offsets, shifts))

    pl.semaphore_wait(barrier, 6 + 2 * (SLABS - 1))

    gather = Gather(vols, VOL_PARTS, vol_send, vol_recv, place)
    gather.start()

    def pair_copy(source, target, n):
        return pltpu.make_async_remote_copy(
            src_ref=source,
            dst_ref=target,
            send_sem=pair_send.at[n],
            recv_sem=pair_recv.at[n],
            device_id={"xband": pair},
            device_id_type=MESH,
        )

    def slab_copy(source, target, n, to, of=band):
        return pltpu.make_async_remote_copy(
            src_ref=source,
            dst_ref=target,
            send_sem=slab_send.at[n],
            recv_sem=slab_recv.at[n],
            device_id={"zslab": slabs[to], "xband": of},
            device_id_type=MESH,
        )

    pair_values = pair_copy(vols.at[0, pl.ds(VOL_ROWS - 8, 8)], pair_vmem, 0)
    pair_values.start()
    seen_up = slab_copy(seen.at[:, pl.ds(ROWS, 8)], seen.at[:, pl.ds(0, 8)], 0, 1)
    seen_down = slab_copy(seen.at[:, pl.ds(8, 8)], seen.at[:, pl.ds(ROWS + 8, 8)], 1, SLABS - 1)
    seen_up.start()
    seen_down.start()

    for t in range(TILES):
        image[t, 0:8, :] = zeros
        image[t, 8 + ROWS :, :] = zeros
        for q in range(2):
            proj[q, t] = jnp.zeros((EXT, 128), jnp.float32)
            back[q, t] = jnp.zeros((ROWS, 128), jnp.float32)

    def fill_own(n, carry):
        angle = half * COLUMN + n
        tap_tables(mag_ref[angle], offset_ref[angle].astype(jnp.float32), index_ref, weight_ref, 2 * n)
        return carry

    lax.fori_loop(0, COLUMN, fill_own, 0)

    def fill_pair():
        pair_values.wait_recv()
        local = pltpu.make_async_copy(pair_vmem, pair_ref, table_sem.at[COLUMN])
        local.start()
        local.wait()

        def one(n, carry):
            angle = half * COLUMN + n
            tap_tables(pair_ref[0, angle], pair_ref[1, angle], index_ref, weight_ref, 2 * n + 1)
            return carry

        lax.fori_loop(0, COLUMN, one, 0)

    def table_copy(slot):
        return pltpu.make_async_copy(
            vols.at[slot, pl.ds(VOL_ROWS - 8, 8)], tables.at[slot], table_sem.at[slot]
        )

    def project(slot):
        table_copy(slot).wait()

        def one(q, carry):
            angle = band + q * (pair - band)
            shift = jnp.clip(tables[slot, 2, angle].astype(jnp.int32), -HALO, HALO)
            total = load_total(proj, q, EXT)
            project_block(vols, slot, tables[slot, 0, angle], tables[slot, 1, angle], shift, image, total)
            store_total(proj, q, total)
            return carry

        lax.fori_loop(0, 2, one, 0)

    gather.run(lambda slot: table_copy(slot).start(), project, fill_pair)

    exchange = [
        pair_copy(proj.at[1], other, 1),
        slab_copy(proj.at[0, :, pl.ds(ROWS, 8)], below.at[0], 2, 1),
        slab_copy(proj.at[0, :, pl.ds(0, 8)], above.at[0], 3, SLABS - 1),
        slab_copy(proj.at[1, :, pl.ds(ROWS, 8)], below.at[1], 4, 1, pair),
        slab_copy(proj.at[1, :, pl.ds(0, 8)], above.at[1], 5, SLABS - 1, pair),
    ]
    for copy in exchange:
        copy.start()
    for q in range(2):
        for t in range(TILES):
            column = jnp.zeros((1, 128), jnp.float32)
            for g in range(EXT // 8):
                value = proj[q, t, 8 * g : 8 * g + 8, :]
                if g == 0:
                    value = jnp.where(row + slab * ROWS >= HALO, value, 0.0)
                if g == EXT // 8 - 1:
                    value = jnp.where((row < HALO) | (slab < SLABS - 1), value, 0.0)
                column = column + jnp.sum(value, axis=0, keepdims=True)
            own_sums[q, t : t + 1, :] = column
            if q == 0:
                column = jnp.sum(seen[t, 8 : 8 + ROWS, :], axis=0, keepdims=True)
            else:
                column = jnp.zeros((1, 128), jnp.float32)
            own_sums[q, TILES + t : TILES + t + 1, :] = column
        for j in range(1 - q, SLABS):
            n = 5 + j + 7 * q + q
            if j == 0:
                copy = pair_copy(own_sums.at[1], sums.at[SLABS], 2)
            else:
                copy = slab_copy(own_sums.at[q], sums.at[SLABS * q + j], n, j, pair if q else band)
            copy.start()
            exchange.append(copy)
    for copy in [seen_up, seen_down] + exchange:
        copy.wait_recv()

    all_sums = own_sums[0]
    for j in range(1, 2 * SLABS):
        all_sums = all_sums + sums[j]
    for t in range(TILES):
        gain = all_sums[TILES + t : TILES + t + 1, :] / all_sums[t : t + 1, :]
        gain = jnp.broadcast_to(gain, (8, 128))
        for g in range(EXT // 8):
            value = proj[0, t, 8 * g : 8 * g + 8, :] + other[t, 8 * g : 8 * g + 8, :]
            if g == 0:
                value = value + jnp.where(slab > 0, below[0, t] + below[1, t], 0.0)
            if g == EXT // 8 - 1:
                value = value + jnp.where(slab < SLABS - 1, above[0, t] + above[1, t], 0.0)
            value = (seen[t, 8 * g + HALO : 8 * g + HALO + 8, :] - gain * value) * (1.0 / BANDS)
            if g == 0:
                value = jnp.where(row + slab * ROWS >= HALO, value, 0.0)
            if g == EXT // 8 - 1:
                value = jnp.where((row < HALO) | (slab < SLABS - 1), value, 0.0)
            ext[t, 8 * g : 8 * g + 8, :] = value
    double = 2 * (lane & 63)
    for k in range(2):
        for phase in range(2):
            for g in range(EXT // 8):
                a = take(ext[2 * k, 8 * g : 8 * g + 8, :], double + phase)
                b = take(ext[2 * k + 1, 8 * g : 8 * g + 8, :], double + phase)
                first = 2 * EXT * k + EXT * phase + 8 * g
                ress[0, first : first + 8, :] = jnp.where(lane < 64, a, b)

    spread_out = Gather(ress, RES_PARTS, res_send, res_recv, place)
    spread_out.start()
    for t in range(TILES):
        residual_ref[0, :, 128 * t : 128 * (t + 1)] = ext[t, HALO : HALO + ROWS, :]

    def backproject(slot):
        r, from_core = slot % 8, core if slot < 8 else 1 - core
        away = -r if r <= 4 else r - 4
        local = lax.rem(z + away * (1 - 2 * from_core) + 2 * RING, RING) * 2 + from_core
        angle = half * COLUMN + local

        def one(q, carry):
            shift = jnp.where(q == 0, shift_ref[angle], pair_ref[2, angle].astype(jnp.int32))
            shift = jnp.clip(shift, -HALO, HALO)
            total = load_total(back, q, ROWS)
            backproject_block(ress, slot, 2 * local + q, shift, index_ref, weight_ref, rows, total)
            store_total(back, q, total)
            return carry

        lax.fori_loop(0, 2, one, 0)

    spread_out.run(lambda slot: None, backproject, lambda: None)
    last = pair_copy(back.at[1], other_back, 3)
    last.start()
    last.wait_recv()
    for t in range(TILES):
        value = (back[0, t] + other_back[t]) * (1.0 / math.sqrt(BANDS))
        correction_ref[0, :, 128 * t : 128 * (t + 1)] = value
    gather.finish()
    spread_out.finish()
    for copy in [pair_values, seen_up, seen_down, last] + exchange:
        copy.wait_send()


def shards(volume, measured, magnification, shift_y, shift_z):
    smem, vmem = pl.BlockSpec(memory_space=pltpu.SMEM), pl.BlockSpec(memory_space=pltpu.VMEM)
    block = jax.ShapeDtypeStruct(volume.shape, jnp.float32)
    f32 = jnp.float32
    return pl.pallas_call(
        kernel,
        out_shape=(block, block),
        in_specs=[smem, smem, smem, vmem, vmem],
        out_specs=(vmem, vmem),
        scratch_shapes=[
            pltpu.VMEM((COLUMN, VOL_ROWS, 128), f32),
            pltpu.VMEM((COLUMN, RES_ROWS, 128), f32),
            pltpu.SMEM((COLUMN, 8, 128), f32),
            pltpu.VMEM((8, 128), f32),
            pltpu.SMEM((8, 128), f32),
            pltpu.VMEM((TILES, ROWS + 16, 128), f32),
            pltpu.VMEM((2, TILES, EXT, 128), f32),
            pltpu.VMEM((TILES, EXT, 128), f32),
            pltpu.VMEM((TILES, EXT, 128), f32),
            pltpu.VMEM((2, TILES, ROWS, 128), f32),
            pltpu.VMEM((TILES, ROWS, 128), f32),
            pltpu.VMEM((2, 8, 128), f32),
            pltpu.VMEM((2 * SLABS, 8, 128), f32),
            pltpu.VMEM((2, TILES, 8, 128), f32),
            pltpu.VMEM((2, TILES, 8, 128), f32),
            pltpu.VMEM((BANDS, 128, 128), jnp.int32),
            pltpu.VMEM((BANDS, 128, 128), f32),
            pltpu.VMEM((TILES, ROWS + 16, 128), f32),
            pltpu.VMEM((RES_ROWS, 128), f32),
            pltpu.SemaphoreType.DMA((COPIES,)),
            pltpu.SemaphoreType.DMA((COPIES,)),
            pltpu.SemaphoreType.DMA((COPIES,)),
            pltpu.SemaphoreType.DMA((COPIES,)),
            pltpu.SemaphoreType.DMA((2 * SLABS + 5,)),
            pltpu.SemaphoreType.DMA((2 * SLABS + 5,)),
            pltpu.SemaphoreType.DMA((4,)),
            pltpu.SemaphoreType.DMA((4,)),
            pltpu.SemaphoreType.DMA((COLUMN + 1,)),
        ],
        compiler_params=pltpu.CompilerParams(
            collective_id=0, has_side_effects=True, vmem_limit_bytes=40 * 1024 * 1024
        ),
        name="sirt",
    )(
        magnification.reshape(BANDS),
        shift_y.reshape(BANDS),
        shift_z.reshape(BANDS),
        volume,
        measured,
    )


def solution(mesh):
    return jax.shard_map(
        shards,
        mesh=mesh,
        in_specs=(
            P("xband", "zslab", None),
            P("xband", "zslab", None),
            P(None, "xband"),
            P(None, "xband"),
            P(None, "xband"),
        ),
        out_specs=(P("xband", "zslab", None), P("xband", "zslab", None)),
        check_vma=False,
    )
```

time: 68.3 us -> 56.4 us (0.83)
  Pallas kernels: 63.9 us -> 51.3 us
    pallas_call x1, Pallas kernels: 63.9 us -> 51.3 us  [shards(): pl.pallas_call(kernel, out_shape=(block, block), in_specs=[smem, smem, sm...]
where the time goes in v2:
time: 56.4 us; the launch traced here: 55.6 us
  Pallas kernels  51.3 us (91%)
  local copies, waits for them, and re-layouts  3.6 us (6%)
  between operations  0.67 us (1%)
    pallas_call x1, Pallas kernels, shards(): pl.pallas_call(kernel, out_shape=(block, block), in_specs=[smem, smem, sm...  51.3 us
    unnamed x12, local copies, waits for them, and re-layouts  3.6 us

profile of v2, /device:TPU:1, one launch (start us, length us, event | category | flops | bytes accessed | tf_op | source)
XLA Modules:
  0.0 55.6 jit_solution(18381796334308733221)
XLA Ops:
  0.6 0.0 copy-start.2
  0.6 0.0 copy-start.3
  0.7 0.0 copy-start.4
  0.7 0.6 %copy-done.2 = f32[32,1]{0,1:T(1,128)S(1)} copy-done((f32[32,1]{0,1:T(1,128)S(1)}, f32[32,1]{0,1:T(1,128)}, u32[]{:S(2)}) %copy-start.2) | copy-done | bytes 152
  1.3 0.0 copy-done.3
  1.3 0.0 copy-done.4
  1.3 0.0 copy-start
  1.3 0.8 %copy-done = f32[1,32,512]{2,1,0:T(8,128)S(1)} copy-done((f32[1,32,512]{2,1,0:T(8,128)S(1)}, f32[1,32,512]{2,1,0:T(8,128)}, u32[]{:S(2)}) %copy-start) | copy-done | bytes 65560
  2.2 0.0 copy-start.1
  2.2 0.8 %copy-done.1 = f32[1,32,512]{2,1,0:T(8,128)S(1)} copy-done((f32[1,32,512]{2,1,0:T(8,128)S(1)}, f32[1,32,512]{2,1,0:T(8,128)}, u32[]{:S(2)}) %copy-start.1) | copy-done | bytes 65560
  3.0 51.3 %sirt.1 = (f32[1,32,512]{2,1,0:T(8,128)S(1)}, f32[1,32,512]{2,1,0:T(8,128)S(1)}) custom-call(f32[32]{0:T(128)S(1)} %bitcast.3, s32[32]{0:T(128)S(1)} %bitcast.4, s32[32]{0:T(128)S(1)} %bitcast.5, f32[1,32,512]{2,1,0:T(8,128)S(1)} %copy-done, f32[1,32,512]{2,1,0:T(8,128)S(1)} %copy-done.1), custom_call_target="tpu_custom_call" | custom-call | tf_op jit(solution)/shard_map/sirt/pallas_call | solution.py:421
  54.3 0.6 %copy.9 = f32[1,32,512]{2,1,0:T(8,128)} copy(f32[1,32,512]{2,1,0:T(8,128)S(1)} %get-tuple-element.4) | data formatting | bytes 131072
  54.9 0.6 %copy.10 = f32[1,32,512]{2,1,0:T(8,128)} copy(f32[1,32,512]{2,1,0:T(8,128)S(1)} %get-tuple-element.5) | data formatting | bytes 131072
Async XLA Ops:
  0.6 0.7 %copy-start.2 = (f32[32,1]{0,1:T(1,128)S(1)}, f32[32,1]{0,1:T(1,128)}, u32[]{:S(2)}) copy-start(f32[32,1]{0,1:T(1,128)} %param.7) | copy-start | bytes 388
  0.6 0.7 %copy-start.3 = (s32[32,1]{0,1:T(1,128)S(1)}, s32[32,1]{0,1:T(1,128)}, u32[]{:S(2)}) copy-start(s32[32,1]{0,1:T(1,128)} %param.8) | copy-start | bytes 388
  0.7 0.7 %copy-start.4 = (s32[32,1]{0,1:T(1,128)S(1)}, s32[32,1]{0,1:T(1,128)}, u32[]{:S(2)}) copy-start(s32[32,1]{0,1:T(1,128)} %param.9) | copy-start | bytes 388
  1.3 0.8 %copy-start = (f32[1,32,512]{2,1,0:T(8,128)S(1)}, f32[1,32,512]{2,1,0:T(8,128)}, u32[]{:S(2)}) copy-start(f32[1,32,512]{2,1,0:T(8,128)} %volume_ref.1) | copy-start | bytes 196612
  2.2 0.8 %copy-start.1 = (f32[1,32,512]{2,1,0:T(8,128)S(1)}, f32[1,32,512]{2,1,0:T(8,128)}, u32[]{:S(2)}) copy-start(f32[1,32,512]{2,1,0:T(8,128)} %measured_ref.1) | copy-start | bytes 196612

commit v3 on v2

v3 whole, which is shorter than its diff:
```python
import functools
import math

import jax
import jax.numpy as jnp
from jax import lax
from jax.experimental import pallas as pl
from jax.experimental.pallas import tpu as pltpu
from jax.sharding import PartitionSpec as P

HALO = 4
TILES = 4
ROWS = 32
EXT = ROWS + 2 * HALO
SLABS = 8
RING = 8
BANDS = 32
CENTRE = 255.5
RES_ROWS = TILES * EXT
VOL_PARTS = ((0, 16), (16, 16), (0, 32))
RES_PARTS = ((0, 80), (80, 80), (0, 160))
COPIES = 20
COLUMN = 16
FORWARD_TILES = ((0, 1), (0, 1, 2), (1, 2, 3), (2, 3))
BACKWARD_TILES = ((0,), (0, 1), (0, 1), (1,))
MESH = pl.DeviceIdType.MESH


def take(x, index):
    return jnp.take_along_axis(x, index, axis=1, mode="promise_in_bounds")


def iota(axis):
    return lax.broadcasted_iota(jnp.int32, (8, 128), axis)


def take_tiles(tiles, index):
    lanes = index & 127
    values = None
    for k, groups in tiles.items():
        part = [take(x, lanes) for x in groups]
        if values is None:
            values = part
        else:
            here = index >= 128 * k
            values = [jnp.where(here, p, v) for p, v in zip(part, values)]
    return values


def project_block(blocks, slot, mag, offset, shift, work, total):
    lane = iota(1)
    mag = jnp.full((8, 128), mag, jnp.float32)
    for ub in range(TILES):
        u = (lane + 128 * ub).astype(jnp.float32)
        target = (u - CENTRE) / mag + CENTRE + offset
        lower = jnp.floor(target)
        frac = target - lower
        left = lower.astype(jnp.int32)
        tiles = {
            k: [blocks[slot, 8 * g : 8 * g + 8, 128 * k : 128 * k + 128] for g in range(ROWS // 8)]
            for k in FORWARD_TILES[ub]
        }
        a = take_tiles(tiles, left)
        b = take_tiles(tiles, left + 1)
        for g in range(ROWS // 8):
            work[ub, 8 + 8 * g : 16 + 8 * g, :] = (1.0 - frac) * a[g] + frac * b[g]
    for ub in range(TILES):
        for rg in range(EXT // 8):
            moved = work[ub, pl.ds(8 + 8 * rg - HALO - shift, 8), :]
            total[ub][rg] = total[ub][rg] + moved


def tap_tables(mag, offset, index_ref, weight_ref, angle):
    lane = iota(1)
    mag = jnp.full((8, 128), mag, jnp.float32)
    for yb in range(TILES):
        y = (lane + 128 * yb).astype(jnp.float32)
        middle = (y - CENTRE - offset) * mag + CENTRE
        for phase in range(2):
            first = jnp.floor((middle - phase) * 0.5).astype(jnp.int32)
            for tap in range(2):
                j = first + tap
                u = (2 * j + phase).astype(jnp.float32)
                target = (u - CENTRE) / mag + CENTRE + offset
                weight = jnp.maximum(0.0, 1.0 - jnp.abs(y - target))
                weight = jnp.where((j >= 0) & (j < 256), weight, 0.0)
                n = 8 * (yb * 4 + phase * 2 + tap)
                index_ref[angle, n : n + 8, :] = jnp.clip(j, 0, 255)
                weight_ref[angle, n : n + 8, :] = weight


def backproject_block(angle, shift, index_ref, weight_ref, work, total):
    for yb in range(TILES):
        for phase in range(2):
            start = EXT * phase + HALO + shift
            tiles = {
                k: [work[pl.ds(start + 2 * EXT * k + 8 * g, 8), :] for g in range(ROWS // 8)]
                for k in BACKWARD_TILES[yb]
            }
            for tap in range(2):
                n = 8 * (4 * yb + 2 * phase + tap)
                values = take_tiles(tiles, index_ref[angle, n : n + 8, :])
                weight = weight_ref[angle, n : n + 8, :]
                total[yb] = [t + weight * v for t, v in zip(total[yb], values)]


OWN = (0, 2, 3, 4, 5, 10, 11, 12)
OTHER = (1, 6, 7, 8, 9, 13, 14, 15)
AWAY = (0, 1, -1, 2, -2, 3, -3, 4)


class Gather:
    def __init__(self, blocks, parts, send, recv, place, own=None):
        self.blocks, self.parts, self.send_sem, self.recv_sem = blocks, parts, send, recv
        self.place = place
        self.own = blocks.at[0] if own is None else own
        self.sent = []

    def copy(self, source, target, part, n, to):
        rows = pl.ds(*self.parts[part])
        return pltpu.make_async_remote_copy(
            src_ref=source.at[rows],
            dst_ref=self.blocks.at[target, rows],
            send_sem=self.send_sem.at[n],
            recv_sem=self.recv_sem.at[n],
            device_id={"xband": self.place[to]},
            device_id_type=MESH,
        )

    def send(self, source, target, part, n, to):
        self.copy(self.blocks.at[source] if source else self.own, target, part, n, to).start()
        self.sent.append((source, target, part, n, to))

    def wait(self, slot, part, n):
        self.copy(self.blocks.at[slot], slot, part, n, "core").wait_recv()

    def start(self):
        for part in range(2):
            self.send(0, OWN[3], part, 2 + part, "long2")
            self.send(0, OWN[4], part, 4 + part, "short2")
        self.send(0, OWN[1], 2, 0, "long1")
        self.send(0, OWN[2], 2, 1, "short1")
        self.core(0)

    def core(self, p):
        self.send(OWN[p], OTHER[p], 2, 12 + p, "core")

    def from_core(self, p):
        self.wait(OTHER[p], 2, 12 + p)

    def run(self, compute, between):
        def first():
            for part in range(2):
                self.wait(OWN[3], part, 2 + part)
                self.send(OWN[3], OWN[7], part, 8 + part, "long2")
                self.send(OWN[3], OWN[5], part, 6 + part, "long1")
                self.wait(OWN[4], part, 4 + part)
                self.send(OWN[4], OWN[6], part, 10 + part, "short1")
            self.core(3)
            self.core(4)
            for n, p in enumerate((1, 2)):
                self.wait(OWN[p], 2, n)
                self.core(p)
            between()
            self.from_core(0)

        def last():
            for p, n in ((5, 6), (6, 10), (7, 8)):
                self.wait(OWN[p], 0, n)
                self.wait(OWN[p], 1, n + 1)
                self.core(p)

        actions = {1: first, OWN[5]: last}
        for p in range(1, RING):
            actions[OTHER[p]] = functools.partial(self.from_core, p)

        def one(slot, carry):
            for n, action in actions.items():
                pl.when(slot == n)(action)
            compute(slot)
            return carry

        lax.fori_loop(0, COLUMN, one, 0)

    def finish(self):
        for source, *rest in self.sent:
            self.copy(self.blocks.at[source] if source else self.own, *rest).wait_send()


def load_total(ref, q, rows):
    return [[ref[q, t, 8 * g : 8 * g + 8, :] for g in range(rows // 8)] for t in range(TILES)]


def store_total(ref, q, total):
    for t, groups in enumerate(total):
        for g, value in enumerate(groups):
            ref[q, t, 8 * g : 8 * g + 8, :] = value


def kernel(
    mag_hbm, offset_hbm, shift_hbm, volume_ref, measured_ref, residual_ref, correction_ref,
    mag_ref, offset_ref, shift_ref, order,
    vols, ress, tables_vmem, tables, pair_vmem, pair_ref, seen, proj, other, ext, back, other_back, own_sums, sums,
    below, above, index_ref, weight_ref, image_0, image_1, rows,
    vol_send, vol_recv, res_send, res_recv, slab_send, slab_recv, pair_send, pair_recv,
    values_send, values_recv, local_sem,
):
    slab, band = lax.axis_index("zslab"), lax.axis_index("xband")
    half, core = lax.div(band, 16), lax.rem(band, 2)
    z = lax.div(lax.rem(band, 16), 2)
    turn = 1 - 2 * core
    pair = (1 - half) * COLUMN + lax.rem(band, COLUMN)

    def ring(away, core=core):
        return half * COLUMN + lax.rem(z + away + 2 * RING, RING) * 2 + core

    scalars = [
        pltpu.make_async_copy(source, target, local_sem.at[n])
        for n, (source, target) in enumerate(
            ((mag_hbm, mag_ref), (offset_hbm, offset_ref), (shift_hbm, shift_ref))
        )
    ]
    own_block = pltpu.make_async_copy(volume_ref.at[0], vols.at[0], local_sem.at[3])
    own_seen = [
        pltpu.make_async_copy(
            measured_ref.at[0, :, pl.ds(128 * t, 128)], seen.at[t, pl.ds(8, ROWS)], local_sem.at[4 + t]
        )
        for t in range(TILES)
    ]
    for copy in [*scalars, own_block, *own_seen]:
        copy.start()

    place = {
        "long1": ring(turn),
        "long2": ring(2 * turn),
        "short1": ring(-turn),
        "short2": ring(-2 * turn),
        "core": band + turn,
        "pair": pair,
    }
    column = {}
    for p, away in enumerate(AWAY):
        column[OWN[p]], column[OTHER[p]] = ring(turn * away), ring(turn * away, 1 - core)
    del column[0]
    for p, away in enumerate(AWAY):
        order[OWN[p]] = lax.rem(z - turn * away + 2 * RING, RING) * 2 + core
        order[OTHER[p]] = lax.rem(z + turn * away + 2 * RING, RING) * 2 + 1 - core
    barrier = pltpu.get_barrier_semaphore()
    for to in [*column.values(), pair]:
        pl.semaphore_signal(barrier, inc=1, device_id={"xband": to}, device_id_type=MESH)
    slabs = [lax.rem(slab + j, SLABS) for j in range(SLABS)]
    for to in slabs[1:]:
        for of in (band, pair):
            pl.semaphore_signal(barrier, inc=1, device_id={"zslab": to, "xband": of}, device_id_type=MESH)

    lane, row = iota(1), iota(0)
    for copy in scalars:
        copy.wait()

    def spread(angle, values):
        here = lane == angle
        mags, offsets, shifts = values
        return (
            jnp.where(here, mag_ref[angle], mags),
            jnp.where(here, offset_ref[angle].astype(jnp.float32), offsets),
            jnp.where(here, shift_ref[angle].astype(jnp.float32), shifts),
        )

    zeros = jnp.zeros((8, 128), jnp.float32)
    mags, offsets, shifts = lax.fori_loop(0, BANDS, spread, (zeros, zeros, zeros))
    tables_vmem[0] = jnp.where(row == 0, mags, jnp.where(row == 1, offsets, shifts))

    pl.semaphore_wait(barrier, COLUMN + 2 * (SLABS - 1))

    gather = Gather(vols, VOL_PARTS, vol_send, vol_recv, place, volume_ref.at[0])
    gather.start()

    def pair_copy(source, target, n):
        return pltpu.make_async_remote_copy(
            src_ref=source,
            dst_ref=target,
            send_sem=pair_send.at[n],
            recv_sem=pair_recv.at[n],
            device_id={"xband": pair},
            device_id_type=MESH,
        )

    def slab_copy(source, target, n, to, of=band):
        return pltpu.make_async_remote_copy(
            src_ref=source,
            dst_ref=target,
            send_sem=slab_send.at[n],
            recv_sem=slab_recv.at[n],
            device_id={"zslab": slabs[to], "xband": of},
            device_id_type=MESH,
        )

    pair_values = pair_copy(tables_vmem.at[0], pair_vmem, 0)
    pair_values.start()
    values = [
        pltpu.make_async_remote_copy(
            src_ref=tables_vmem.at[0],
            dst_ref=tables_vmem.at[r],
            send_sem=values_send.at[r],
            recv_sem=values_recv.at[r],
            device_id={"xband": to},
            device_id_type=MESH,
        )
        for r, to in column.items()
    ]
    for copy in values:
        copy.start()
    own_table = pltpu.make_async_copy(tables_vmem.at[0], tables.at[0], local_sem.at[0])
    own_table.start()
    for copy in own_seen:
        copy.wait()
    seen_up = slab_copy(seen.at[:, pl.ds(ROWS, 8)], seen.at[:, pl.ds(0, 8)], 0, 1)
    seen_down = slab_copy(seen.at[:, pl.ds(8, 8)], seen.at[:, pl.ds(ROWS + 8, 8)], 1, SLABS - 1)
    seen_up.start()
    seen_down.start()

    for t in range(TILES):
        for image in (image_0, image_1):
            image[t, 0:8, :] = zeros
            image[t, 8 + ROWS :, :] = zeros
        for q in range(2):
            proj[q, t] = jnp.zeros((EXT, 128), jnp.float32)
            back[q, t] = jnp.zeros((ROWS, 128), jnp.float32)

    def fill_own(n, carry):
        angle = half * COLUMN + order[n]
        tap_tables(mag_ref[angle], offset_ref[angle].astype(jnp.float32), index_ref, weight_ref, 2 * n)
        return carry

    lax.fori_loop(0, COLUMN, fill_own, 0)

    def between():
        for copy in [pair_values, *values]:
            copy.wait_recv()
        local = [
            pltpu.make_async_copy(pair_vmem, pair_ref, local_sem.at[1]),
            pltpu.make_async_copy(
                tables_vmem.at[pl.ds(1, COLUMN - 1)], tables.at[pl.ds(1, COLUMN - 1)], local_sem.at[2]
            ),
        ]
        for copy in local:
            copy.start()
        for copy in local:
            copy.wait()

    def fill_pair():
        def one(n, carry):
            angle = half * COLUMN + order[n]
            tap_tables(pair_ref[0, angle], pair_ref[1, angle], index_ref, weight_ref, 2 * n + 1)
            return carry

        lax.fori_loop(0, COLUMN, one, 0)

    def project(slot):
        for q in range(2):
            angle = pair if q else band
            mag, offset, shift = (tables[slot, n, angle] for n in range(3))
            shift = jnp.clip(shift.astype(jnp.int32), -HALO, HALO)
            total = load_total(proj, q, EXT)
            project_block(vols, slot, mag, offset, shift, image_1 if q else image_0, total)
            store_total(proj, q, total)

    own_block.wait()
    own_table.wait()
    gather.run(project, between)

    exchange = [
        pair_copy(proj.at[1], other, 1),
        slab_copy(proj.at[0, :, pl.ds(ROWS, 8)], below.at[0], 2, 1),
        slab_copy(proj.at[0, :, pl.ds(0, 8)], above.at[0], 3, SLABS - 1),
        slab_copy(proj.at[1, :, pl.ds(ROWS, 8)], below.at[1], 4, 1, pair),
        slab_copy(proj.at[1, :, pl.ds(0, 8)], above.at[1], 5, SLABS - 1, pair),
    ]
    for copy in exchange:
        copy.start()
    for q in range(2):
        for t in range(TILES):
            column = jnp.zeros((1, 128), jnp.float32)
            for g in range(EXT // 8):
                value = proj[q, t, 8 * g : 8 * g + 8, :]
                if g == 0:
                    value = jnp.where(row + slab * ROWS >= HALO, value, 0.0)
                if g == EXT // 8 - 1:
                    value = jnp.where((row < HALO) | (slab < SLABS - 1), value, 0.0)
                column = column + jnp.sum(value, axis=0, keepdims=True)
            own_sums[q, t : t + 1, :] = column
            if q == 0:
                column = jnp.sum(seen[t, 8 : 8 + ROWS, :], axis=0, keepdims=True)
            else:
                column = jnp.zeros((1, 128), jnp.float32)
            own_sums[q, TILES + t : TILES + t + 1, :] = column
        for j in range(1 - q, SLABS):
            n = 5 + j + 7 * q + q
            if j == 0:
                copy = pair_copy(own_sums.at[1], sums.at[SLABS], 2)
            else:
                copy = slab_copy(own_sums.at[q], sums.at[SLABS * q + j], n, j, pair if q else band)
            copy.start()
            exchange.append(copy)
    fill_pair()
    for copy in [seen_up, seen_down] + exchange:
        copy.wait_recv()

    all_sums = own_sums[0]
    for j in range(1, 2 * SLABS):
        all_sums = all_sums + sums[j]
    for t in range(TILES):
        gain = all_sums[TILES + t : TILES + t + 1, :] / all_sums[t : t + 1, :]
        gain = jnp.broadcast_to(gain, (8, 128))
        for g in range(EXT // 8):
            value = proj[0, t, 8 * g : 8 * g + 8, :] + other[t, 8 * g : 8 * g + 8, :]
            if g == 0:
                value = value + jnp.where(slab > 0, below[0, t] + below[1, t], 0.0)
            if g == EXT // 8 - 1:
                value = value + jnp.where(slab < SLABS - 1, above[0, t] + above[1, t], 0.0)
            value = (seen[t, 8 * g + HALO : 8 * g + HALO + 8, :] - gain * value) * (1.0 / BANDS)
            if g == 0:
                value = jnp.where(row + slab * ROWS >= HALO, value, 0.0)
            if g == EXT // 8 - 1:
                value = jnp.where((row < HALO) | (slab < SLABS - 1), value, 0.0)
            ext[t, 8 * g : 8 * g + 8, :] = value
    double = 2 * (lane & 63)
    for k in range(2):
        for phase in range(2):
            for g in range(EXT // 8):
                a = take(ext[2 * k, 8 * g : 8 * g + 8, :], double + phase)
                b = take(ext[2 * k + 1, 8 * g : 8 * g + 8, :], double + phase)
                first = 2 * EXT * k + EXT * phase + 8 * g
                ress[0, first : first + 8, :] = jnp.where(lane < 64, a, b)

    spread_out = Gather(ress, RES_PARTS, res_send, res_recv, place)
    spread_out.start()
    for t in range(TILES):
        residual_ref[0, :, 128 * t : 128 * (t + 1)] = ext[t, HALO : HALO + ROWS, :]

    def backproject(slot):
        angle = half * COLUMN + order[slot]
        for n in range(0, RES_ROWS, 8):
            rows[n : n + 8, :] = ress[slot, n : n + 8, :]
        for q in range(2):
            shift = pair_ref[2, angle].astype(jnp.int32) if q else shift_ref[angle]
            total = load_total(back, q, ROWS)
            backproject_block(2 * slot + q, jnp.clip(shift, -HALO, HALO), index_ref, weight_ref, rows, total)
            store_total(back, q, total)

    spread_out.run(backproject, lambda: None)
    last = pair_copy(back.at[1], other_back, 3)
    last.start()
    last.wait_recv()
    for t in range(TILES):
        value = (back[0, t] + other_back[t]) * (1.0 / math.sqrt(BANDS))
        correction_ref[0, :, 128 * t : 128 * (t + 1)] = value
    gather.finish()
    spread_out.finish()
    for copy in [pair_values, *values, seen_up, seen_down, last, *exchange]:
        copy.wait_send()


def shards(volume, measured, magnification, shift_y, shift_z):
    hbm, vmem = pl.BlockSpec(memory_space=pltpu.HBM), pl.BlockSpec(memory_space=pltpu.VMEM)
    block = jax.ShapeDtypeStruct(volume.shape, jnp.float32)
    f32 = jnp.float32
    return pl.pallas_call(
        kernel,
        out_shape=(block, block),
        in_specs=[hbm] * 5,
        out_specs=(vmem, vmem),
        scratch_shapes=[
            pltpu.SMEM((BANDS,), f32),
            pltpu.SMEM((BANDS,), jnp.int32),
            pltpu.SMEM((BANDS,), jnp.int32),
            pltpu.SMEM((COLUMN,), jnp.int32),
            pltpu.VMEM((COLUMN, ROWS, 128 * TILES), f32),
            pltpu.VMEM((COLUMN, RES_ROWS, 128), f32),
            pltpu.VMEM((COLUMN, 8, 128), f32),
            pltpu.SMEM((COLUMN, 8, 128), f32),
            pltpu.VMEM((8, 128), f32),
            pltpu.SMEM((8, 128), f32),
            pltpu.VMEM((TILES, ROWS + 16, 128), f32),
            pltpu.VMEM((2, TILES, EXT, 128), f32),
            pltpu.VMEM((TILES, EXT, 128), f32),
            pltpu.VMEM((TILES, EXT, 128), f32),
            pltpu.VMEM((2, TILES, ROWS, 128), f32),
            pltpu.VMEM((TILES, ROWS, 128), f32),
            pltpu.VMEM((2, 8, 128), f32),
            pltpu.VMEM((2 * SLABS, 8, 128), f32),
            pltpu.VMEM((2, TILES, 8, 128), f32),
            pltpu.VMEM((2, TILES, 8, 128), f32),
            pltpu.VMEM((BANDS, 128, 128), jnp.int32),
            pltpu.VMEM((BANDS, 128, 128), f32),
            pltpu.VMEM((TILES, ROWS + 16, 128), f32),
            pltpu.VMEM((TILES, ROWS + 16, 128), f32),
            pltpu.VMEM((RES_ROWS, 128), f32),
            pltpu.SemaphoreType.DMA((COPIES,)),
            pltpu.SemaphoreType.DMA((COPIES,)),
            pltpu.SemaphoreType.DMA((COPIES,)),
            pltpu.SemaphoreType.DMA((COPIES,)),
            pltpu.SemaphoreType.DMA((2 * SLABS + 5,)),
            pltpu.SemaphoreType.DMA((2 * SLABS + 5,)),
            pltpu.SemaphoreType.DMA((4,)),
            pltpu.SemaphoreType.DMA((4,)),
            pltpu.SemaphoreType.DMA((COLUMN,)),
            pltpu.SemaphoreType.DMA((COLUMN,)),
            pltpu.SemaphoreType.DMA((4 + TILES,)),
        ],
        compiler_params=pltpu.CompilerParams(
            collective_id=0, has_side_effects=True, vmem_limit_bytes=62 * 1024 * 1024
        ),
        name="sirt",
    )(
        magnification.reshape(BANDS),
        shift_y.reshape(BANDS),
        shift_z.reshape(BANDS),
        volume,
        measured,
    )


def solution(mesh):
    return jax.shard_map(
        shards,
        mesh=mesh,
        in_specs=(
            P("xband", "zslab", None),
            P("xband", "zslab", None),
            P(None, "xband"),
            P(None, "xband"),
            P(None, "xband"),
        ),
        out_specs=(P("xband", "zslab", None), P("xband", "zslab", None)),
        check_vma=False,
    )
```

time: 56.4 us -> 54.9 us (0.973); the launches traced: 55.6 us -> 54.8 us
  local copies, waits for them, and re-layouts: 3.6 us -> 2.14 us
  Pallas kernels: 51.3 us -> 52 us
    unnamed x12 -> x4, local copies, waits for them, and re-layouts: 3.6 us -> 2.14 us
    pallas_call x1, Pallas kernels: 51.3 us -> 52 us  [shards(): pl.pallas_call(kernel, out_shape=(block, block), in_specs=[hbm] * 5, out_...]
where the time goes in v3:
time: 54.9 us; the launch traced here: 54.8 us
  Pallas kernels  52 us (95%)
  local copies, waits for them, and re-layouts  2.14 us (4%)
  between operations  0.65 us (1%)
    pallas_call x1, Pallas kernels, shards(): pl.pallas_call(kernel, out_shape=(block, block), in_specs=[hbm] * 5, out_...  52 us
    unnamed x4, local copies, waits for them, and re-layouts  2.14 us

profile of v3, /device:TPU:1, one launch (start us, length us, event | category | flops | bytes accessed | tf_op | source)
XLA Modules:
  0.0 54.8 jit_solution(17251542636231041199)
XLA Ops:
  0.6 52.0 %sirt.1 = (f32[1,32,512]{2,1,0:T(8,128)}, f32[1,32,512]{2,1,0:T(8,128)}) custom-call(f32[32]{0:T(128)} %bitcast.3, s32[32]{0:T(128)} %bitcast.4, s32[32]{0:T(128)} %bitcast.5, f32[1,32,512]{2,1,0:T(8,128)} %volume_ref.1, f32[1,32,512]{2,1,0:T(8,128)} %measured_ref.1), custom_call_target="tpu_custom_call" | custom-call | tf_op jit(solution)/shard_map/sirt/pallas_call | solution.py:468
  52.6 0.0 copy-start
  52.6 1.5 %copy.9 = f32[1,32,512]{2,1,0:T(8,128)} copy(f32[1,32,512]{2,1,0:T(8,128)} %get-tuple-element.4) | data formatting | bytes 131072
  54.1 0.0 copy-done
  54.1 0.6 %copy.10 = f32[1,32,512]{2,1,0:T(8,128)} copy(f32[1,32,512]{2,1,0:T(8,128)S(1)} %copy-done) | data formatting | bytes 131072
Async XLA Ops:
  52.6 1.5 %copy-start = (f32[1,32,512]{2,1,0:T(8,128)S(1)}, f32[1,32,512]{2,1,0:T(8,128)}, u32[]{:S(2)}) copy-start(f32[1,32,512]{2,1,0:T(8,128)} %get-tuple-element.5) | copy-start | bytes 196612

commit v4 on v3

v4 whole, which is shorter than its diff:
```python
import functools
import math

import jax
import jax.numpy as jnp
from jax import lax
from jax.experimental import pallas as pl
from jax.experimental.pallas import tpu as pltpu
from jax.sharding import PartitionSpec as P

HALO = 4
TILES = 4
ROWS = 32
EXT = ROWS + 2 * HALO
SLABS = 8
RING = 8
BANDS = 32
CENTRE = 255.5
RES_ROWS = TILES * ROWS
VOL_PARTS = ((0, 16), (16, 16), (0, 32))
RES_PARTS = ((0, 64), (64, 64), (0, 128))
COPIES = 20
COLUMN = 16
FORWARD_TILES = ((0, 1), (0, 1, 2), (1, 2, 3), (2, 3))
BACKWARD_TILES = ((0,), (0, 1), (0, 1), (1,))
MESH = pl.DeviceIdType.MESH


def take(x, index):
    return jnp.take_along_axis(x, index, axis=1, mode="promise_in_bounds")


def iota(axis):
    return lax.broadcasted_iota(jnp.int32, (8, 128), axis)


def take_tiles(tiles, index):
    lanes = index & 127
    values = None
    for k, groups in tiles.items():
        part = [take(x, lanes) for x in groups]
        if values is None:
            values = part
        else:
            here = index >= 128 * k
            values = [jnp.where(here, p, v) for p, v in zip(part, values)]
    return values


def moved(work, tile, shift, total):
    return [t + work[tile, pl.ds(8 + 8 * g - HALO - shift, 8), :] for g, t in enumerate(total)]


def project_tile(blocks, slot, ub, mag, offset, shift, work, total):
    mag = jnp.full((8, 128), mag, jnp.float32)
    u = (iota(1) + 128 * ub).astype(jnp.float32)
    target = (u - CENTRE) / mag + CENTRE + offset
    lower = jnp.floor(target)
    frac = target - lower
    left = lower.astype(jnp.int32)
    tiles = {
        k: [blocks[slot, 8 * g : 8 * g + 8, 128 * k : 128 * k + 128] for g in range(ROWS // 8)]
        for k in FORWARD_TILES[ub]
    }
    a = take_tiles(tiles, left)
    b = take_tiles(tiles, left + 1)
    for g in range(ROWS // 8):
        work[ub, 8 + 8 * g : 16 + 8 * g, :] = (1.0 - frac) * a[g] + frac * b[g]
    return moved(work, ub, shift, total)


def tap_tables(mag, offset, index_ref, weight_ref, angle):
    lane = iota(1)
    mag = jnp.full((8, 128), mag, jnp.float32)
    for yb in range(TILES):
        y = (lane + 128 * yb).astype(jnp.float32)
        middle = (y - CENTRE - offset) * mag + CENTRE
        for phase in range(2):
            first = jnp.floor((middle - phase) * 0.5).astype(jnp.int32)
            for tap in range(2):
                j = first + tap
                u = (2 * j + phase).astype(jnp.float32)
                target = (u - CENTRE) / mag + CENTRE + offset
                weight = jnp.maximum(0.0, 1.0 - jnp.abs(y - target))
                weight = jnp.where((j >= 0) & (j < 256), weight, 0.0)
                n = 8 * (yb * 4 + phase * 2 + tap)
                index_ref[angle, n : n + 8, :] = jnp.clip(j, 0, 255)
                weight_ref[angle, n : n + 8, :] = weight


def backproject_tile(blocks, slot, yb, angle, shift, index_ref, weight_ref, work, total):
    image = [jnp.zeros((8, 128), jnp.float32)] * (ROWS // 8)
    for phase in range(2):
        tiles = {}
        for k in BACKWARD_TILES[yb]:
            start = ROWS * (2 * k + phase)
            tiles[k] = [blocks[slot, start + 8 * g : start + 8 * g + 8, :] for g in range(ROWS // 8)]
        for tap in range(2):
            n = 8 * (4 * yb + 2 * phase + tap)
            values = take_tiles(tiles, index_ref[angle, n : n + 8, :])
            weight = weight_ref[angle, n : n + 8, :]
            image = [i + weight * v for i, v in zip(image, values)]
    for g, value in enumerate(image):
        work[yb, 8 + 8 * g : 16 + 8 * g, :] = value
    return moved(work, yb, -shift, total)


OWN = (0, 2, 3, 4, 5, 10, 11, 12)
OTHER = (1, 6, 7, 8, 9, 13, 14, 15)
AWAY = (0, 1, -1, 2, -2, 3, -3, 4)


class Gather:
    def __init__(self, blocks, parts, send, recv, place, own=None):
        self.blocks, self.parts, self.send_sem, self.recv_sem = blocks, parts, send, recv
        self.place = place
        self.own = blocks.at[0] if own is None else own
        self.sent = []

    def copy(self, source, target, part, n, to):
        rows = pl.ds(*self.parts[part])
        return pltpu.make_async_remote_copy(
            src_ref=source.at[rows],
            dst_ref=self.blocks.at[target, rows],
            send_sem=self.send_sem.at[n],
            recv_sem=self.recv_sem.at[n],
            device_id={"xband": self.place[to]},
            device_id_type=MESH,
        )

    def send(self, source, target, part, n, to):
        self.copy(self.blocks.at[source] if source else self.own, target, part, n, to).start()
        self.sent.append((source, target, part, n, to))

    def wait(self, slot, part, n):
        self.copy(self.blocks.at[slot], slot, part, n, "core").wait_recv()

    def start(self):
        for part in range(2):
            self.send(0, OWN[3], part, 2 + part, "long2")
            self.send(0, OWN[4], part, 4 + part, "short2")
        self.send(0, OWN[1], 2, 0, "long1")
        self.send(0, OWN[2], 2, 1, "short1")
        self.core(0)

    def core(self, p):
        self.send(OWN[p], OTHER[p], 2, 12 + p, "core")

    def from_core(self, p):
        self.wait(OTHER[p], 2, 12 + p)

    def run(self, compute, finish, hooks=None):
        hooks = hooks or {}
        def first():
            if "first" in hooks:
                hooks["first"]()
            for part in range(2):
                self.wait(OWN[3], part, 2 + part)
                self.send(OWN[3], OWN[7], part, 8 + part, "long2")
                self.send(OWN[3], OWN[5], part, 6 + part, "long1")
                self.wait(OWN[4], part, 4 + part)
                self.send(OWN[4], OWN[6], part, 10 + part, "short1")
                if "far" in hooks and part == 0:
                    hooks["far"]()
            self.core(3)
            self.core(4)
            for n, p in enumerate((1, 2)):
                self.wait(OWN[p], 2, n)
                self.core(p)
            self.from_core(0)

        def last():
            for p, n in ((5, 6), (6, 10), (7, 8)):
                self.wait(OWN[p], 0, n)
                self.wait(OWN[p], 1, n + 1)
                self.core(p)

        actions = {1: first, OWN[5]: last}
        for p in range(1, RING - 1):
            actions[OTHER[p]] = functools.partial(self.from_core, p)

        def one(slot, carry):
            for n, action in actions.items():
                pl.when(slot == n)(action)
                if n in hooks:
                    pl.when(slot == n)(hooks[n])
            compute(slot)
            return carry

        lax.fori_loop(0, COLUMN - 1, one, 0)
        self.from_core(RING - 1)
        finish(COLUMN - 1)

    def finish(self):
        for source, *rest in self.sent:
            self.copy(self.blocks.at[source] if source else self.own, *rest).wait_send()


def load_total(ref, q, t):
    return [ref[q, t, 8 * g : 8 * g + 8, :] for g in range(EXT // 8)]


def store_total(ref, q, t, total):
    for g, value in enumerate(total):
        ref[q, t, 8 * g : 8 * g + 8, :] = value


def kernel(
    mag_hbm, offset_hbm, shift_hbm, volume_ref, measured_ref, residual_ref, correction_ref,
    mag_ref, offset_ref, shift_ref, order,
    vols, ress, tables_vmem, tables, pair_vmem, pair_ref, seen, proj, back, other, ext, own_sums, sums,
    below, above, index_ref, weight_ref, image_0, image_1,
    vol_send, vol_recv, res_send, res_recv, slab_send, slab_recv, pair_send, pair_recv,
    values_send, values_recv, local_sem, word_sem,
):
    slab, band = lax.axis_index("zslab"), lax.axis_index("xband")
    half, core = lax.div(band, 16), lax.rem(band, 2)
    z = lax.div(lax.rem(band, 16), 2)
    turn = 1 - 2 * core
    pair = (1 - half) * COLUMN + lax.rem(band, COLUMN)

    def ring(away, core=core):
        return half * COLUMN + lax.rem(z + away + 2 * RING, RING) * 2 + core

    scalars = [
        pltpu.make_async_copy(source, target, local_sem.at[n])
        for n, (source, target) in enumerate(
            ((mag_hbm, mag_ref), (offset_hbm, offset_ref), (shift_hbm, shift_ref))
        )
    ]
    own_block = pltpu.make_async_copy(volume_ref.at[0], vols.at[0], local_sem.at[3])
    own_seen = pltpu.make_async_copy(measured_ref.at[0], seen, local_sem.at[4])
    for copy in [*scalars, own_block, own_seen]:
        copy.start()

    place = {
        "long1": ring(turn),
        "long2": ring(2 * turn),
        "short1": ring(-turn),
        "short2": ring(-2 * turn),
        "core": band + turn,
        "pair": pair,
    }
    for p, away in enumerate(AWAY):
        order[OWN[p]] = lax.rem(z - turn * away + 2 * RING, RING) * 2 + core
        order[OTHER[p]] = lax.rem(z + turn * away + 2 * RING, RING) * 2 + 1 - core
    barrier = pltpu.get_barrier_semaphore()
    for to in place.values():
        pl.semaphore_signal(barrier, inc=1, device_id={"xband": to}, device_id_type=MESH)
    slabs = [lax.rem(slab + j, SLABS) for j in range(SLABS)]
    for to in (slabs[1], slabs[SLABS - 1]):
        for of in (band, pair):
            pl.semaphore_signal(barrier, inc=1, device_id={"zslab": to, "xband": of}, device_id_type=MESH)

    pl.semaphore_wait(barrier, len(place) + 4)

    gather = Gather(vols, VOL_PARTS, vol_send, vol_recv, place, volume_ref.at[0])
    gather.start()

    lane, row = iota(1), iota(0)
    for copy in scalars:
        copy.wait()

    def spread(angle, values):
        here = lane == angle
        mags, offsets, shifts = values
        return (
            jnp.where(here, mag_ref[angle], mags),
            jnp.where(here, offset_ref[angle].astype(jnp.float32), offsets),
            jnp.where(here, shift_ref[angle].astype(jnp.float32), shifts),
        )

    zeros = jnp.zeros((8, 128), jnp.float32)
    mags, offsets, shifts = lax.fori_loop(0, BANDS, spread, (zeros, zeros, zeros))
    tables_vmem[0] = jnp.where(row == 0, mags, jnp.where(row == 1, offsets, shifts))

    def tell(n):
        for side, to in enumerate((slabs[n + 1], slabs[SLABS - 1 - n])):
            pl.semaphore_signal(word_sem.at[n, side], inc=1, device_id={"zslab": to}, device_id_type=MESH)

    def hear(n):
        for side in range(2):
            pl.semaphore_wait(word_sem.at[n, side], 1)

    tell(0)

    def pair_copy(source, target, n):
        return pltpu.make_async_remote_copy(
            src_ref=source,
            dst_ref=target,
            send_sem=pair_send.at[n],
            recv_sem=pair_recv.at[n],
            device_id={"xband": pair},
            device_id_type=MESH,
        )

    def slab_copy(source, target, n, to, of=band):
        return pltpu.make_async_remote_copy(
            src_ref=source,
            dst_ref=target,
            send_sem=slab_send.at[n],
            recv_sem=slab_recv.at[n],
            device_id={"zslab": slabs[to], "xband": of},
            device_id_type=MESH,
        )

    pair_values = pair_copy(tables_vmem.at[0], pair_vmem, 0)
    pair_values.start()
    def values_copy(source, target, to):
        return pltpu.make_async_remote_copy(
            src_ref=tables_vmem.at[source],
            dst_ref=tables_vmem.at[target],
            send_sem=values_send.at[target],
            recv_sem=values_recv.at[target],
            device_id={"xband": place[to]},
            device_id_type=MESH,
        )

    routes = (
        (0, OWN[3], "long2"), (0, OWN[4], "short2"), (0, OWN[1], "long1"), (0, OWN[2], "short1"),
        (OWN[3], OWN[7], "long2"), (OWN[3], OWN[5], "long1"), (OWN[4], OWN[6], "short1"),
        *((OWN[p], OTHER[p], "core") for p in range(RING)),
    )
    for route in (*routes[:4], routes[7]):
        values_copy(*route).start()

    def values_on(p):
        values_copy(0, OWN[p], "core").wait_recv()
        for route in routes:
            if route[0] == OWN[p]:
                values_copy(*route).start()

    def to_smem(first, count, n):
        rows = pl.ds(first, count)
        return pltpu.make_async_copy(tables_vmem.at[rows], tables.at[rows], local_sem.at[n])

    own_table = pltpu.make_async_copy(tables_vmem.at[0], tables.at[0], local_sem.at[0])
    own_table.start()
    for t in range(TILES):
        for image in (image_0, image_1):
            image[t, 0:8, :] = zeros
            image[t, 8 + ROWS :, :] = zeros
        for q in range(2):
            proj[q, t] = jnp.zeros((EXT, 128), jnp.float32)
            back[q, t] = jnp.zeros((EXT, 128), jnp.float32)

    def fill_own(n, carry):
        angle = half * COLUMN + order[n]
        tap_tables(mag_ref[angle], offset_ref[angle].astype(jnp.float32), index_ref, weight_ref, 2 * n)
        return carry

    lax.fori_loop(0, COLUMN, fill_own, 0)

    def near_values():
        pair_values.wait_recv()
        local = pltpu.make_async_copy(pair_vmem, pair_ref, local_sem.at[1])
        local.start()
        for p in (1, 2):
            values_on(p)
        values_copy(0, OTHER[0], "core").wait_recv()
        near = to_smem(1, 5, 2)
        near.start()
        near.wait()
        local.wait()

    def core_values():
        for p in range(1, 5):
            values_copy(0, OTHER[p], "core").wait_recv()
        core = to_smem(OTHER[1], 4, 2)
        core.start()
        core.wait()

    def far_values():
        for p in (5, 6, 7):
            values_on(p)

    def last_values():
        for p in (5, 6, 7):
            values_copy(0, OTHER[p], "core").wait_recv()
        far = to_smem(OWN[5], 6, 2)
        far.start()
        far.wait()

    def fill_pair():
        def one(n, carry):
            angle = half * COLUMN + order[n]
            tap_tables(pair_ref[0, angle], pair_ref[1, angle], index_ref, weight_ref, 2 * n + 1)
            return carry

        lax.fori_loop(0, COLUMN, one, 0)

    images = (image_0, image_1)
    exchanged = []

    def start(copy):
        copy.start()
        exchanged.append(copy)

    def tiles_apart(ref, tile, phase, after):
        def finish(slot):
            for q in (1, 0):
                values = tile(slot, q)
                for t in range(TILES):
                    store_total(ref, q, t, values(t, load_total(ref, q, t)))
                    if q:
                        start(pair_copy(ref.at[1, t], other.at[phase, t], 2 + TILES * phase + t))
                of, n = (pair, 4 * phase + 2) if q else (band, 4 * phase)
                start(slab_copy(ref.at[q, :, pl.ds(ROWS, 8)], below.at[phase, q], n, 1, of))
                start(slab_copy(ref.at[q, :, pl.ds(0, 8)], above.at[phase, q], n + 1, SLABS - 1, of))
                after(q)

        return finish

    def each(ref, tile):
        def compute(slot):
            for q in range(2):
                values = tile(slot, q)
                for t in range(TILES):
                    store_total(ref, q, t, values(t, load_total(ref, q, t)))

        return compute

    def full_rows(ref, t, phase):
        for g in range(EXT // 8):
            value = ref[0, t, 8 * g : 8 * g + 8, :] + other[phase, t, 8 * g : 8 * g + 8, :]
            if g == 0:
                value = value + jnp.where(slab > 0, below[phase, 0, t] + below[phase, 1, t], 0.0)
            if g == EXT // 8 - 1:
                value = value + jnp.where(slab < SLABS - 1, above[phase, 0, t] + above[phase, 1, t], 0.0)
            ext[t, 8 * g : 8 * g + 8, :] = value

    def project(slot, q):
        angle = pair if q else band
        mag, offset, shift = (tables[slot, n, angle] for n in range(3))
        shift = jnp.clip(shift.astype(jnp.int32), -HALO, HALO)
        return lambda t, total: project_tile(vols, slot, t, mag, offset, shift, images[q], total)

    def send_sums(q):
        for t in range(TILES):
            column = jnp.zeros((1, 128), jnp.float32)
            for g in range(EXT // 8):
                value = proj[q, t, 8 * g : 8 * g + 8, :]
                if g == 0:
                    value = jnp.where(row + slab * ROWS >= HALO, value, 0.0)
                if g == EXT // 8 - 1:
                    value = jnp.where((row < HALO) | (slab < SLABS - 1), value, 0.0)
                column = column + jnp.sum(value, axis=0, keepdims=True)
            own_sums[q, t : t + 1, :] = column
        if q:
            start(pair_copy(own_sums.at[1], sums.at[SLABS], 1))
        for j in range(1, SLABS):
            start(slab_copy(own_sums.at[q], sums.at[SLABS * q + j], 7 + 7 * q + j, j, pair if q else band))

    own_seen.wait()
    for t in range(TILES):
        column = jnp.sum(seen[:, 128 * t : 128 * t + 128], axis=0, keepdims=True)
        own_sums[0, TILES + t : TILES + t + 1, :] = column
        own_sums[1, TILES + t : TILES + t + 1, :] = jnp.zeros((1, 128), jnp.float32)
    own_block.wait()
    own_table.wait()
    hooks = {
        "first": lambda: [hear(0), tell(1)],
        "far": lambda: [values_on(3), values_on(4)],
        1: near_values,
        6: core_values,
        7: lambda: hear(1),
        8: far_values,
        9: last_values,
    }
    gather.run(each(proj, project), tiles_apart(proj, project, 0, send_sums), hooks)
    fill_pair()
    for copy in exchanged:
        copy.wait_recv()

    all_sums = own_sums[0]
    for j in range(1, 2 * SLABS):
        all_sums = all_sums + sums[j]
    for t in range(TILES):
        full_rows(proj, t, 0)
        gain = all_sums[TILES + t : TILES + t + 1, :] / all_sums[t : t + 1, :]
        gain = jnp.broadcast_to(gain, (8, 128))
        for g in range(ROWS // 8):
            value = seen[8 * g : 8 * g + 8, 128 * t : 128 * t + 128]
            value = value - gain * ext[t, HALO + 8 * g : HALO + 8 * g + 8, :]
            residual_ref[0, 8 * g : 8 * g + 8, 128 * t : 128 * t + 128] = value
    double = 2 * (lane & 63)
    for k in range(2):
        for phase in range(2):
            for g in range(ROWS // 8):
                a = residual_ref[0, 8 * g : 8 * g + 8, 256 * k : 256 * k + 128]
                b = residual_ref[0, 8 * g : 8 * g + 8, 256 * k + 128 : 256 * k + 256]
                first = ROWS * (2 * k + phase) + 8 * g
                value = jnp.where(lane < 64, take(a, double + phase), take(b, double + phase))
                ress[0, first : first + 8, :] = value

    spread_out = Gather(ress, RES_PARTS, res_send, res_recv, place)
    spread_out.start()

    def backproject(slot, q):
        angle = half * COLUMN + order[slot]
        shift = pair_ref[2, angle].astype(jnp.int32) if q else shift_ref[angle]
        shift = jnp.clip(shift, -HALO, HALO)
        return lambda t, total: backproject_tile(
            ress, slot, t, 2 * slot + q, shift, index_ref, weight_ref, images[q], total
        )

    before = len(exchanged)
    spread_out.run(each(back, backproject), tiles_apart(back, backproject, 1, lambda q: None))
    for copy in exchanged[before:]:
        copy.wait_recv()
    for t in range(TILES):
        full_rows(back, t, 1)
        correction_ref[0, :, 128 * t : 128 * (t + 1)] = ext[t, HALO : HALO + ROWS, :]
    gather.finish()
    spread_out.finish()
    for route in routes:
        values_copy(*route).wait_send()
    for copy in [pair_values, *exchanged]:
        copy.wait_send()


def shards(volume, measured, magnification, shift_y, shift_z):
    hbm, vmem = pl.BlockSpec(memory_space=pltpu.HBM), pl.BlockSpec(memory_space=pltpu.VMEM)
    block = jax.ShapeDtypeStruct(volume.shape, jnp.float32)
    f32 = jnp.float32
    residual, correction = pl.pallas_call(
        kernel,
        out_shape=(block, block),
        in_specs=[hbm] * 5,
        out_specs=(vmem, vmem),
        scratch_shapes=[
            pltpu.SMEM((BANDS,), f32),
            pltpu.SMEM((BANDS,), jnp.int32),
            pltpu.SMEM((BANDS,), jnp.int32),
            pltpu.SMEM((COLUMN,), jnp.int32),
            pltpu.VMEM((COLUMN, ROWS, 128 * TILES), f32),
            pltpu.VMEM((COLUMN, RES_ROWS, 128), f32),
            pltpu.VMEM((COLUMN, 8, 128), f32),
            pltpu.SMEM((COLUMN, 8, 128), f32),
            pltpu.VMEM((8, 128), f32),
            pltpu.SMEM((8, 128), f32),
            pltpu.VMEM((ROWS, 128 * TILES), f32),
            pltpu.VMEM((2, TILES, EXT, 128), f32),
            pltpu.VMEM((2, TILES, EXT, 128), f32),
            pltpu.VMEM((2, TILES, EXT, 128), f32),
            pltpu.VMEM((TILES, EXT, 128), f32),
            pltpu.VMEM((2, 8, 128), f32),
            pltpu.VMEM((2 * SLABS, 8, 128), f32),
            pltpu.VMEM((2, 2, TILES, 8, 128), f32),
            pltpu.VMEM((2, 2, TILES, 8, 128), f32),
            pltpu.VMEM((BANDS, 128, 128), jnp.int32),
            pltpu.VMEM((BANDS, 128, 128), f32),
            pltpu.VMEM((TILES, ROWS + 16, 128), f32),
            pltpu.VMEM((TILES, ROWS + 16, 128), f32),
            pltpu.SemaphoreType.DMA((COPIES,)),
            pltpu.SemaphoreType.DMA((COPIES,)),
            pltpu.SemaphoreType.DMA((COPIES,)),
            pltpu.SemaphoreType.DMA((COPIES,)),
            pltpu.SemaphoreType.DMA((22,)),
            pltpu.SemaphoreType.DMA((22,)),
            pltpu.SemaphoreType.DMA((2 + 2 * TILES,)),
            pltpu.SemaphoreType.DMA((2 + 2 * TILES,)),
            pltpu.SemaphoreType.DMA((COLUMN,)),
            pltpu.SemaphoreType.DMA((COLUMN,)),
            pltpu.SemaphoreType.DMA((5,)),
            pltpu.SemaphoreType.REGULAR((2, 2)),
        ],
        compiler_params=pltpu.CompilerParams(
            collective_id=0, has_side_effects=True, vmem_limit_bytes=55040 * 1024
        ),
        name="sirt",
    )(
        magnification.reshape(BANDS),
        shift_y.reshape(BANDS),
        shift_z.reshape(BANDS),
        volume,
        measured,
    )
    return residual * (1.0 / BANDS), correction * (1.0 / (BANDS * math.sqrt(BANDS)))


def solution(mesh):
    return jax.shard_map(
        shards,
        mesh=mesh,
        in_specs=(
            P("xband", "zslab", None),
            P("xband", "zslab", None),
            P(None, "xband"),
            P(None, "xband"),
            P(None, "xband"),
        ),
        out_specs=(P("xband", "zslab", None), P("xband", "zslab", None)),
        check_vma=False,
    )
```

time: 54.9 us -> 53.6 us (0.976)
  local copies, waits for them, and re-layouts: 2.14 us -> 0.66 us
  other arithmetic: 0 us -> 0.66 us
    unnamed x4 -> x6, local copies, waits for them, and re-layouts: 2.14 us -> 0.66 us
    mul x0 -> x1, other arithmetic: none -> 0.66 us  [shards(): correction * (1.0 / (BANDS * math.sqrt(BANDS)))]
where the time goes in v4:
time: 53.6 us; the launch traced here: 53.5 us
  Pallas kernels  51.5 us (96%)
  local copies, waits for them, and re-layouts  0.66 us (1%)
  other arithmetic  0.66 us (1%)
  between operations  0.66 us (1%)
    pallas_call x1, Pallas kernels, shards(): pl.pallas_call(kernel, out_shape=(block, block), in_specs=[hbm] * 5, out_...  51.5 us

profile of v4, /device:TPU:1, one launch (start us, length us, event | category | flops | bytes accessed | tf_op | source)
XLA Modules:
  0.0 53.5 jit_solution(5704551768480116469)
XLA Ops:
  0.6 0.0 copy-start
  0.6 0.0 copy-start.1
  0.7 0.0 copy-start.2
  0.7 0.6 %copy-done = f32[32,1]{0,1:T(1,128)S(1)} copy-done((f32[32,1]{0,1:T(1,128)S(1)}, f32[32,1]{0,1:T(1,128)}, u32[]{:S(2)}) %copy-start) | copy-done | bytes 152
  1.3 0.0 copy-done.1
  1.3 0.0 copy-done.2
  1.3 51.5 %sirt.1 = (f32[1,32,512]{2,1,0:T(8,128)S(1)}, f32[1,32,512]{2,1,0:T(8,128)S(1)}) custom-call(f32[32]{0:T(128)S(1)} %bitcast.3, s32[32]{0:T(128)S(1)} %bitcast.4, s32[32]{0:T(128)S(1)} %bitcast.5, f32[1,32,512]{2,1,0:T(8,128)} %volume_ref.1, f32[1,32,512]{2,1,0:T(8,128)} %measured_ref.1), custom_call_target="tpu_custom_call" | custom-call | tf_op jit(solution)/shard_map/sirt/pallas_call | solution.py:526
  52.8 0.7 %broadcast_multiply_fusion = (f32[1,32,512]{2,1,0:T(8,128)}, f32[1,32,512]{2,1,0:T(8,128)}) fusion(f32[1,32,512]{2,1,0:T(8,128)S(1)} %get-tuple-element.5, f32[1,32,512]{2,1,0:T(8,128)S(1)} %get-tuple-element.4), kind=kLoop, calls=%fused_computation | loop fusion | flops 32768 | bytes 262144 | tf_op jit(solution)/shard_map/mul | solution.py:579
Async XLA Ops:
  0.6 0.7 %copy-start = (f32[32,1]{0,1:T(1,128)S(1)}, f32[32,1]{0,1:T(1,128)}, u32[]{:S(2)}) copy-start(f32[32,1]{0,1:T(1,128)} %param.7) | copy-start | bytes 388
  0.6 0.7 %copy-start.1 = (s32[32,1]{0,1:T(1,128)S(1)}, s32[32,1]{0,1:T(1,128)}, u32[]{:S(2)}) copy-start(s32[32,1]{0,1:T(1,128)} %param.8) | copy-start | bytes 388
  0.7 0.7 %copy-start.2 = (s32[32,1]{0,1:T(1,128)S(1)}, s32[32,1]{0,1:T(1,128)}, u32[]{:S(2)}) copy-start(s32[32,1]{0,1:T(1,128)} %param.9) | copy-start | bytes 388

commit v5 on v4

--- a/solution.py
+++ b/solution.py
@@ -523,6 +523,7 @@
     hbm, vmem = pl.BlockSpec(memory_space=pltpu.HBM), pl.BlockSpec(memory_space=pltpu.VMEM)
     block = jax.ShapeDtypeStruct(volume.shape, jnp.float32)
     f32 = jnp.float32
+    arguments = (*(x.reshape(BANDS) for x in (magnification, shift_y, shift_z)), volume, measured)
     residual, correction = pl.pallas_call(
         kernel,
         out_shape=(block, block),
@@ -566,16 +567,10 @@
             pltpu.SemaphoreType.REGULAR((2, 2)),
         ],
         compiler_params=pltpu.CompilerParams(
-            collective_id=0, has_side_effects=True, vmem_limit_bytes=55040 * 1024
+            collective_id=0, has_side_effects=True, vmem_limit_bytes=40 * 1024 * 1024
         ),
         name="sirt",
-    )(
-        magnification.reshape(BANDS),
-        shift_y.reshape(BANDS),
-        shift_z.reshape(BANDS),
-        volume,
-        measured,
-    )
+    )(*(pltpu.with_memory_space_constraint(x, pltpu.HBM) for x in arguments))
     return residual * (1.0 / BANDS), correction * (1.0 / (BANDS * math.sqrt(BANDS)))
 
 

time: 53.6 us -> 53 us (0.989)
  local copies, waits for them, and re-layouts: 0.66 us -> 0 us
    unnamed x6 -> x0, local copies, waits for them, and re-layouts: 0.66 us -> none
where the time goes in v5:
time: 53 us
  Pallas kernels  51.7 us (98%)
  other arithmetic  0.66 us (1%)
  between operations  0.64 us (1%)
    pallas_call x1, Pallas kernels, shards(): pl.pallas_call(kernel, out_shape=(block, block), in_specs=[hbm] * 5, out_...  51.7 us

profile of v5, /device:TPU:1, one launch (start us, length us, event | category | flops | bytes accessed | tf_op | source)
XLA Modules:
  0.0 53.0 jit_solution(18297300723054795117)
XLA Ops:
  0.6 51.7 %sirt.1 = (f32[1,32,512]{2,1,0:T(8,128)S(1)}, f32[1,32,512]{2,1,0:T(8,128)S(1)}) custom-call(f32[32]{0:T(128)} %bitcast.3, s32[32]{0:T(128)} %bitcast.4, s32[32]{0:T(128)} %bitcast.5, f32[1,32,512]{2,1,0:T(8,128)} %volume_ref.1, f32[1,32,512]{2,1,0:T(8,128)} %measured_ref.1), custom_call_target="tpu_custom_call" | custom-call | tf_op jit(solution)/shard_map/sirt/pallas_call | solution.py:527
  52.3 0.7 %broadcast_multiply_fusion = (f32[1,32,512]{2,1,0:T(8,128)}, f32[1,32,512]{2,1,0:T(8,128)}) fusion(f32[1,32,512]{2,1,0:T(8,128)S(1)} %get-tuple-element.5, f32[1,32,512]{2,1,0:T(8,128)S(1)} %get-tuple-element.4), kind=kLoop, calls=%fused_computation | loop fusion | flops 32768 | bytes 262144 | tf_op jit(solution)/shard_map/mul | solution.py:574

commit v6 on v5

--- a/solution.py
+++ b/solution.py
@@ -156,8 +156,8 @@
                 hooks["first"]()
             for part in range(2):
                 self.wait(OWN[3], part, 2 + part)
+                self.send(OWN[3], OWN[5], part, 6 + part, "long1")
                 self.send(OWN[3], OWN[7], part, 8 + part, "long2")
-                self.send(OWN[3], OWN[5], part, 6 + part, "long1")
                 self.wait(OWN[4], part, 4 + part)
                 self.send(OWN[4], OWN[6], part, 10 + part, "short1")
                 if "far" in hooks and part == 0:
@@ -463,9 +463,9 @@
         "far": lambda: [values_on(3), values_on(4)],
         1: near_values,
         6: core_values,
-        7: lambda: hear(1),
-        8: far_values,
-        9: last_values,
+        14: lambda: hear(1),
+        9: far_values,
+        10: last_values,
     }
     gather.run(each(proj, project), tiles_apart(proj, project, 0, send_sums), hooks)
     fill_pair()

time: 53 us -> 52.2 us (0.985)
  Pallas kernels: 51.7 us -> 50.8 us
    pallas_call x1, Pallas kernels: 51.7 us -> 50.8 us  [shards(): pl.pallas_call(kernel, out_shape=(block, block), in_specs=[hbm] * 5, out_...]
where the time goes in v6:
time: 52.2 us; the launch traced here: 52.1 us
  Pallas kernels  50.8 us (97%)
  other arithmetic  0.66 us (1%)
  between operations  0.64 us (1%)
    pallas_call x1, Pallas kernels, shards(): pl.pallas_call(kernel, out_shape=(block, block), in_specs=[hbm] * 5, out_...  50.8 us

profile of v6, /device:TPU:1, one launch (start us, length us, event | category | flops | bytes accessed | tf_op | source)
XLA Modules:
  0.0 52.1 jit_solution(12171484853333045119)
XLA Ops:
  0.6 50.8 %sirt.1 = (f32[1,32,512]{2,1,0:T(8,128)S(1)}, f32[1,32,512]{2,1,0:T(8,128)S(1)}) custom-call(f32[32]{0:T(128)} %bitcast.3, s32[32]{0:T(128)} %bitcast.4, s32[32]{0:T(128)} %bitcast.5, f32[1,32,512]{2,1,0:T(8,128)} %volume_ref.1, f32[1,32,512]{2,1,0:T(8,128)} %measured_ref.1), custom_call_target="tpu_custom_call" | custom-call | tf_op jit(solution)/shard_map/sirt/pallas_call | solution.py:527
  51.4 0.7 %broadcast_multiply_fusion = (f32[1,32,512]{2,1,0:T(8,128)}, f32[1,32,512]{2,1,0:T(8,128)}) fusion(f32[1,32,512]{2,1,0:T(8,128)S(1)} %get-tuple-element.5, f32[1,32,512]{2,1,0:T(8,128)S(1)} %get-tuple-element.4), kind=kLoop, calls=%fused_computation | loop fusion | flops 32768 | bytes 262144 | tf_op jit(solution)/shard_map/mul | solution.py:574

commit v7 on v6

--- a/solution.py
+++ b/solution.py
@@ -135,10 +135,11 @@
     def wait(self, slot, part, n):
         self.copy(self.blocks.at[slot], slot, part, n, "core").wait_recv()
 
-    def start(self):
-        for part in range(2):
-            self.send(0, OWN[3], part, 2 + part, "long2")
-            self.send(0, OWN[4], part, 4 + part, "short2")
+    def start_part(self, part):
+        self.send(0, OWN[3], part, 2 + part, "long2")
+        self.send(0, OWN[4], part, 4 + part, "short2")
+
+    def start_rest(self):
         self.send(0, OWN[1], 2, 0, "long1")
         self.send(0, OWN[2], 2, 1, "short1")
         self.core(0)
@@ -255,7 +256,9 @@
     pl.semaphore_wait(barrier, len(place) + 4)
 
     gather = Gather(vols, VOL_PARTS, vol_send, vol_recv, place, volume_ref.at[0])
-    gather.start()
+    gather.start_part(0)
+    gather.start_part(1)
+    gather.start_rest()
 
     lane, row = iota(1), iota(0)
     for copy in scalars:
@@ -475,6 +478,8 @@
     all_sums = own_sums[0]
     for j in range(1, 2 * SLABS):
         all_sums = all_sums + sums[j]
+    double = 2 * (lane & 63)
+    spread_out = Gather(ress, RES_PARTS, res_send, res_recv, place)
     for t in range(TILES):
         full_rows(proj, t, 0)
         gain = all_sums[TILES + t : TILES + t + 1, :] / all_sums[t : t + 1, :]
@@ -483,8 +488,9 @@
             value = seen[8 * g : 8 * g + 8, 128 * t : 128 * t + 128]
             value = value - gain * ext[t, HALO + 8 * g : HALO + 8 * g + 8, :]
             residual_ref[0, 8 * g : 8 * g + 8, 128 * t : 128 * t + 128] = value
-    double = 2 * (lane & 63)
-    for k in range(2):
+        if t % 2 == 0:
+            continue
+        k = t // 2
         for phase in range(2):
             for g in range(ROWS // 8):
                 a = residual_ref[0, 8 * g : 8 * g + 8, 256 * k : 256 * k + 128]
@@ -492,9 +498,8 @@
                 first = ROWS * (2 * k + phase) + 8 * g
                 value = jnp.where(lane < 64, take(a, double + phase), take(b, double + phase))
                 ress[0, first : first + 8, :] = value
-
-    spread_out = Gather(ress, RES_PARTS, res_send, res_recv, place)
-    spread_out.start()
+        spread_out.start_part(k)
+    spread_out.start_rest()
 
     def backproject(slot, q):
         angle = half * COLUMN + order[slot]

time: 52.2 us -> 52.2 us (level)
  no operation moved by 1% of the time
where the time goes in v7:
time: 52.2 us; the launch traced here: 52.1 us
  Pallas kernels  50.8 us (97%)
  other arithmetic  0.66 us (1%)
  between operations  0.64 us (1%)
    pallas_call x1, Pallas kernels, shards(): pl.pallas_call(kernel, out_shape=(block, block), in_specs=[hbm] * 5, out_...  50.8 us

profile of v7, /device:TPU:1, one launch (start us, length us, event | category | flops | bytes accessed | tf_op | source)
XLA Modules:
  0.0 52.1 jit_solution(9562039948299567690)
XLA Ops:
  0.6 50.8 %sirt.1 = (f32[1,32,512]{2,1,0:T(8,128)S(1)}, f32[1,32,512]{2,1,0:T(8,128)S(1)}) custom-call(f32[32]{0:T(128)} %bitcast.3, s32[32]{0:T(128)} %bitcast.4, s32[32]{0:T(128)} %bitcast.5, f32[1,32,512]{2,1,0:T(8,128)} %volume_ref.1, f32[1,32,512]{2,1,0:T(8,128)} %measured_ref.1), custom_call_target="tpu_custom_call" | custom-call | tf_op jit(solution)/shard_map/sirt/pallas_call | solution.py:532
  51.4 0.7 %broadcast_multiply_fusion = (f32[1,32,512]{2,1,0:T(8,128)}, f32[1,32,512]{2,1,0:T(8,128)}) fusion(f32[1,32,512]{2,1,0:T(8,128)S(1)} %get-tuple-element.5, f32[1,32,512]{2,1,0:T(8,128)S(1)} %get-tuple-element.4), kind=kLoop, calls=%fused_computation | loop fusion | flops 32768 | bytes 262144 | tf_op jit(solution)/shard_map/mul | solution.py:579
